TPU v7x, 32 devices: a whole 2x2x4 slice. The times are simulated.
32 devices in a mesh: groups: 2 (over y), row: 2 (over x), col: 8 (over z, core).
Axes of the slice: x: 2, y: 2, z: 4, core: 2. Of those that a mesh axis runs over, the one named last changes fastest.
Arguments:
- node_states: bfloat16 [4096, 1024], P(('groups', 'col')), parts along dimension 0, may hold values from -14 to 14
- query_weight: bfloat16 [1024, 1024], P(None, 'row'), may hold values from -1 to 1
- key_weight: bfloat16 [1024, 1024], P(None, 'row'), may hold values from -1 to 1
- value_weight: bfloat16 [1024, 1024], P(None, 'row'), may hold values from -0.1875 to 0.1875
- output_grad: bfloat16 [4096, 1024], P(('groups', 'col'), 'row'), parts along dimension 0, may hold values from -6 to 6
- pair_list: int32 [16, 32, 2], P(('groups', 'col')), parts along dimension 0, may hold values from 0 to 15, as said below
- pair_count: int32 [16], P(('groups', 'col')), parts along dimension 0, may hold values from 2 to 32, as said below
Outputs:
- attended: bfloat16 [4096, 1024], P(('groups', 'col'), 'row'), parts along dimension 0
- node_grad: float32 [4096, 1024], P(('groups', 'col'), 'row'), parts along dimension 0
- query_grad: float32 [2048, 1024], P(('groups', 'col'), 'row'), parts along dimension 0
- key_grad: float32 [2048, 1024], P(('groups', 'col'), 'row'), parts along dimension 0
- value_grad: float32 [2048, 1024], P(('groups', 'col'), 'row'), parts along dimension 0
There are 2 independent parts, one for each index of `groups`. A program takes and returns all parts, laid end to end along the dimension named above; an argument that names none is the same for every part. Nothing has to cross between parts.
Inputs may be any that keep to these rules, and one draw needn't show every extreme that they name: `pair_list`: slot p of panel c holds a query block of the panel and a key block; the first pair_count[c] slots of a panel are distinct pairs and include (q, c * 2 + q) for every query block q; later slots hold valid indices and are not listed. `pair_count`: some panel lists all 32 slots.
All inputs are finite; a program needn't handle non-finite values.
Results may differ from a plain program's by a relative error of at most 0.015.
The roundings to bfloat16 on the way count: a program that leaves them out, or rounds other values in their place, can miss the bound.
Values may be sent and summed in bfloat16 or wider, within the bound.
A program may use at most 192 MiB of HBM per device.

v0:
```python
import math

import jax
import jax.numpy as jnp
from jax import lax
from jax.sharding import PartitionSpec as P

DH = 64
BLK = 128


LOWEST = -1e30
EXACT = lax.Precision.HIGHEST


def slot_batch(pair_rows, pair_total, turn_index, width, blocks):
    start = turn_index * width
    query_block = pair_rows[:, 0]
    key_block = pair_rows[:, 1]
    slot_live = start + jnp.arange(width, dtype=jnp.int32) < pair_total
    owners = jnp.logical_and(
        query_block[:, None] == jnp.arange(blocks, dtype=jnp.int32)[None, :], slot_live[:, None]
    )
    return (query_block, key_block, slot_live, owners)


def batch_tiles(query_tiles, table_tiles, query_block, key_block, head_cols, factor):
    head_count = head_cols // DH
    width = query_block.shape[0]
    query_pick = jnp.take(query_tiles, query_block, axis=0)
    table_pick = jnp.take(table_tiles, key_block, axis=0)
    key_pick = table_pick[:, :, :head_cols].reshape(width, BLK, head_count, DH)
    value_pick = table_pick[:, :, head_cols:].reshape(width, BLK, head_count, DH)
    scores = (
        jnp.einsum("sihd,sjhd->shij", query_pick, key_pick, preferred_element_type=jnp.float32)
        * factor
    )
    return (query_pick, key_pick, value_pick, scores)


def batch_weights(scores, row_top, totals, query_block, slot_live):
    top_pick = jnp.take(row_top, query_block, axis=0)
    total_pick = jnp.take(totals, query_block, axis=0)
    weights = jnp.exp(scores - top_pick[..., None]) / total_pick[..., None]
    return jnp.where(slot_live[:, None, None, None], weights, 0.0).astype(jnp.bfloat16)


def per_device(
    node_states, query_weight, key_weight, value_weight, output_grad, pair_list, pair_count
):
    head_cols = query_weight.shape[1]
    head_count = head_cols // DH
    panel_rows = node_states.shape[0]
    blocks = panel_rows // BLK
    factor = 1.0 / math.sqrt(DH)
    pair_rows = pair_list[0]
    pair_total = pair_count[0]
    width = math.gcd(pair_rows.shape[0], 32)
    turns = (pair_total + width - 1) // width
    queries = jnp.dot(node_states, query_weight, preferred_element_type=jnp.float32).astype(
        jnp.bfloat16
    )
    keys_here = jnp.dot(node_states, key_weight, preferred_element_type=jnp.float32).astype(
        jnp.bfloat16
    )
    values_here = jnp.dot(node_states, value_weight, preferred_element_type=jnp.float32).astype(
        jnp.bfloat16
    )
    local_table = jnp.concatenate([keys_here, values_here], axis=1)
    key_table = lax.all_gather(local_table, "col", axis=0, tiled=True)
    key_blocks_all = key_table.shape[0] // BLK
    query_tiles = queries.reshape(blocks, BLK, head_count, DH)
    table_tiles = key_table.reshape(key_blocks_all, BLK, 2 * head_cols)

    def stats_turn(turn_index, state_pair):
        row_top, totals = state_pair
        query_block, key_block, slot_live, owners = slot_batch(
            pair_rows, pair_total, turn_index, width, blocks
        )
        scores = batch_tiles(query_tiles, table_tiles, query_block, key_block, head_cols, factor)[3]
        pair_top = jnp.max(scores, axis=3)
        block_top = jnp.max(jnp.where(owners[:, :, None, None], pair_top[:, None], LOWEST), axis=0)
        new_top = jnp.maximum(row_top, block_top)
        top_pick = jnp.take(new_top, query_block, axis=0)
        exp_terms = jnp.where(
            slot_live[:, None, None, None], jnp.exp(scores - top_pick[..., None]), 0.0
        )
        added = jnp.einsum(
            "sn,shi->nhi", owners.astype(jnp.float32), jnp.sum(exp_terms, axis=3), precision=EXACT
        )
        totals = totals * jnp.exp(row_top - new_top) + added
        return (new_top, totals)

    start_top = jnp.full((blocks, head_count, BLK), LOWEST, jnp.float32)
    start_total = jnp.zeros((blocks, head_count, BLK), jnp.float32)
    row_top, totals = lax.fori_loop(0, turns, stats_turn, (start_top, start_total))

    def attend_turn(turn_index, output):
        query_block, key_block, slot_live, owners = slot_batch(
            pair_rows, pair_total, turn_index, width, blocks
        )
        query_pick, key_pick, value_pick, scores = batch_tiles(
            query_tiles, table_tiles, query_block, key_block, head_cols, factor
        )
        weights = batch_weights(scores, row_top, totals, query_block, slot_live)
        update = jnp.einsum(
            "shij,sjhd->sihd", weights, value_pick, preferred_element_type=jnp.float32
        )
        return output + jnp.einsum(
            "sn,sihd->nihd", owners.astype(jnp.float32), update, precision=EXACT
        )

    output = lax.fori_loop(
        0, turns, attend_turn, jnp.zeros((blocks, BLK, head_count, DH), jnp.float32)
    )
    attended = output.reshape(panel_rows, head_cols).astype(jnp.bfloat16)
    grad_tiles = output_grad.reshape(blocks, BLK, head_count, DH)
    deltas = jnp.sum(grad_tiles.astype(jnp.float32) * output, axis=3)
    back_table = lax.all_gather(local_table, "col", axis=0, tiled=True)
    back_tiles = back_table.reshape(key_blocks_all, BLK, 2 * head_cols)

    def backward_turn(turn_index, state_pair):
        grad_rows, key_grads = state_pair
        query_block, key_block, slot_live, owners = slot_batch(
            pair_rows, pair_total, turn_index, width, blocks
        )
        query_pick, key_pick, value_pick, scores = batch_tiles(
            query_tiles, back_tiles, query_block, key_block, head_cols, factor
        )
        weights = batch_weights(scores, row_top, totals, query_block, slot_live)
        grad_pick = jnp.take(grad_tiles, query_block, axis=0)
        value_part = jnp.einsum(
            "shij,sihd->sjhd", weights, grad_pick, preferred_element_type=jnp.float32
        )
        prob_grad = jnp.einsum(
            "sihd,sjhd->shij", grad_pick, value_pick, preferred_element_type=jnp.float32
        )
        delta_pick = jnp.transpose(jnp.take(deltas, query_block, axis=0), (0, 2, 1))
        score_grad = (weights.astype(jnp.float32) * (prob_grad - delta_pick[..., None])).astype(
            jnp.bfloat16
        )
        query_part = (
            jnp.einsum("shij,sjhd->sihd", score_grad, key_pick, preferred_element_type=jnp.float32)
            * factor
        )
        key_part = (
            jnp.einsum(
                "shij,sihd->sjhd", score_grad, query_pick, preferred_element_type=jnp.float32
            )
            * factor
        )
        grad_rows = grad_rows + jnp.einsum(
            "sn,sihd->nihd", owners.astype(jnp.float32), query_part, precision=EXACT
        )
        rows_update = jnp.concatenate(
            [key_part.reshape(width, BLK, head_cols), value_part.reshape(width, BLK, head_cols)],
            axis=2,
        )
        key_grads = key_grads + jax.ops.segment_sum(
            rows_update, key_block, num_segments=key_blocks_all
        )
        return (grad_rows, key_grads)

    start_rows = jnp.zeros((blocks, BLK, head_count, DH), jnp.float32)
    start_keys = jnp.zeros((key_blocks_all, BLK, 2 * head_cols), jnp.float32)
    grad_rows, key_grads = lax.fori_loop(0, turns, backward_turn, (start_rows, start_keys))
    key_grads = key_grads.reshape(key_blocks_all * BLK, 2 * head_cols)
    pair_grads = lax.psum_scatter(
        key_grads.astype(jnp.bfloat16), "col", scatter_dimension=0, tiled=True
    ).astype(jnp.float32)
    query_rows_grad = grad_rows.reshape(panel_rows, head_cols).astype(jnp.bfloat16)
    key_rows_grad = pair_grads[:, :head_cols].astype(jnp.bfloat16)
    value_rows_grad = pair_grads[:, head_cols:].astype(jnp.bfloat16)
    contract = (((1,), (1,)), ((), ()))
    partial_sum = lax.dot_general(
        query_rows_grad, query_weight, contract, preferred_element_type=jnp.float32
    )
    partial_sum = partial_sum + lax.dot_general(
        key_rows_grad, key_weight, contract, preferred_element_type=jnp.float32
    )
    partial_sum = partial_sum + lax.dot_general(
        value_rows_grad, value_weight, contract, preferred_element_type=jnp.float32
    )
    node_grad = lax.psum_scatter(
        partial_sum.astype(jnp.bfloat16), "row", scatter_dimension=1, tiled=True
    ).astype(jnp.float32)
    over_nodes = (((0,), (0,)), ((), ()))
    query_term = lax.dot_general(
        node_states, query_rows_grad, over_nodes, preferred_element_type=jnp.float32
    )
    key_term = lax.dot_general(
        node_states, key_rows_grad, over_nodes, preferred_element_type=jnp.float32
    )
    value_term = lax.dot_general(
        node_states, value_rows_grad, over_nodes, preferred_element_type=jnp.float32
    )
    query_grad, key_grad, value_grad = (
        lax.psum_scatter(
            query_term.astype(jnp.bfloat16), "col", scatter_dimension=0, tiled=True
        ).astype(jnp.float32),
        lax.psum_scatter(
            key_term.astype(jnp.bfloat16), "col", scatter_dimension=0, tiled=True
        ).astype(jnp.float32),
        lax.psum_scatter(
            value_term.astype(jnp.bfloat16), "col", scatter_dimension=0, tiled=True
        ).astype(jnp.float32),
    )
    return (attended, node_grad, query_grad, key_grad, value_grad)


def solution(mesh):
    return jax.shard_map(
        per_device,
        mesh=mesh,
        in_specs=(
            P(("groups", "col"), None),
            P(None, "row"),
            P(None, "row"),
            P(None, "row"),
            P(("groups", "col"), "row"),
            P(("groups", "col"), None, None),
            P(("groups", "col")),
        ),
        out_specs=(
            P(("groups", "col"), "row"),
            P(("groups", "col"), "row"),
            P(("groups", "col"), "row"),
            P(("groups", "col"), "row"),
            P(("groups", "col"), "row"),
        ),
        check_vma=False,
    )
```

profile of v0, /device:TPU:0, one launch (start us, length us, event | category | flops | bytes accessed | tf_op | source)
XLA Modules:
  0.0 593.2 jit_solution(17759031465043939440)
XLA Ops:
  16.7 45.1 %all-gather.2.cloned.1.call-done = bf16[2048,1024]{1,0:T(8,128)(2,1)} async-done(((bf16[256,1024]{1,0:T(8,128)(2,1)}), bf16[2048,1024]{1,0:T(8,128)(2,1)}) %all-gather.2.cloned.1.call-update) | async-done | bytes 4194320 | tf_op jit(solution)/shard_map/all_gather | solution.py:70
  61.9 55.4 %while.34 = (s32[]{:T(128)}, f32[2,8,128]{2,0,1:T(2,128)S(1)}, f32[2,8,128]{2,0,1:T(2,128)S(1)}, s32[]{:T(128)}, s32[32,2]{0,1:T(2,128)S(1)}, /*index=5*/s32[]{:...) while((s32[]{:T(128)}, f32[2,8,128]{2,0,1:T(2,128)S(1)}, ...), condition=%wide.region_4.8_spmd, body=%wide.region_0.7_spmd.sunk | while | flops 567124544 | bytes 93563064 | solution.py:96
  62.7 7.2 %gather_fusion = bf16[32,128,1024]{2,1,0:T(8,128)(2,1)} fusion(bf16[16,128,1024]{2,1,0:T(8,128)(2,1)} %get-tuple-element.694, s32[1024]{0:T(1024)S(1)} %pad_clamp_fusion.14), kind=kCustom, calls=%fused_computation.1.clone.clone.1 | custom fusion | bytes 16777344 | tf_op jit(solution)/shard_map/while/body/jit(_take)/gather | solution.py:31
  85.8 7.5 %broadcast_select_fusion.19 = bf16[32,128,8,64]{3,2,1,0:T(8,128)(2,1)} fusion(bf16[32,128,8,64]{3,2,1,0:T(8,128)(2,1)} %gather_fusion.1, pred[32]{0:T(512)(128)(4,1)S(1)} %get-tuple-element.619), kind=kLoop, calls=%fused_computation.18.clone.1 | loop fusion | flops 2097152 | bytes 8388640 | tf_op jit(solution)/shard_map/while/body/jit(_take)/select_n | solution.py:30
  93.3 12.3 %multiply_reduce_fusion.3 = (f32[32,8,128]{2,1,0:T(8,128)S(1)}, f32[32,8,128,128]{2,3,1,0:T(8,128)}) fusion(bf16[32,128,8,64]{1,3,2,0:T(8,128)(2,1)} %bitcast.184, bf16[32,128,8,64]{3,2,1,0:T(8,128)(2,1)} %broadcast_select_fusion.19), kind=kOutput, calls=%fused_computation.15.clone.1 | convolution fusion | flops 545226752 | bytes 25296896 | tf_op jit(solution)/shard_map/while/body/sihd,sjhd->shij/dot_general | solution.py:35
  106.4 10.7 %select_reduce_fusion.5 = f32[32,8,128]{2,1,0:T(8,128)S(1)} fusion(f32[32,8,128,128]{2,3,1,0:T(8,128)} %get-tuple-element.622, f32[32,8,128]{2,1,0:T(8,128)S(1)} %broadcast_select_fusion.20, pred[32]{0:T(512)(128)(4,1)S(1)} %get-tuple-element.621), kind=kLoop, calls=%fused_computation.14.clone.1 | loop fusion | flops 16744448 | bytes 17039392 | tf_op jit(solution)/shard_map/while/body/reduce_sum | solution.py:89
  117.5 91.5 %while.35 = (s32[]{:T(128)}, f32[2,128,8,64]{1,0,3,2:T(2,128)S(1)}, s32[]{:T(128)}, s32[32,2]{0,1:T(2,128)S(1)}, s32[]{:T(128)}, /*index=5*/bf16[16,128,1024]{2,...) while((s32[]{:T(128)}, f32[2,128,8,64]{1,0,3,2:T(2,128)S(1)}, ...), condition=%wide.region_6.10_spmd, body=%wide.region_5.9_spmd.sunk | while | flops 1151535744 | bytes 115615744 | solution.py:113
  124.7 7.5 %broadcast_select_fusion.22 = bf16[32,128,8,64]{3,2,1,0:T(8,128)(2,1)} fusion(bf16[32,128,8,64]{3,2,1,0:T(8,128)(2,1)} %gather_fusion.4, pred[32]{0:T(512)(128)(4,1)S(1)} %get-tuple-element.637), kind=kLoop, calls=%fused_computation.39.clone.1 | loop fusion | flops 2097152 | bytes 8388640 | tf_op jit(solution)/shard_map/while/body/jit(_take)/select_n | solution.py:30
  132.2 7.2 %gather_fusion.3 = bf16[32,128,1024]{2,1,0:T(8,128)(2,1)} fusion(bf16[16,128,1024]{2,1,0:T(8,128)(2,1)} %get-tuple-element.724, s32[1024]{0:T(1024)S(1)} %pad_clamp_fusion.16), kind=kCustom, calls=%fused_computation.6.clone.clone.1 | custom fusion | bytes 16777344 | tf_op jit(solution)/shard_map/while/body/jit(_take)/gather | solution.py:31
  139.4 7.5 %broadcast_select_fusion.21 = bf16[32,128,1024]{2,1,0:T(8,128)(2,1)} fusion(bf16[32,128,1024]{2,1,0:T(8,128)(2,1)} %gather_fusion.3, pred[32]{0:T(512)(128)(4,1)S(1)} %get-tuple-element.633), kind=kLoop, calls=%fused_computation.40.clone.1 | loop fusion | flops 4194304 | bytes 16777248 | tf_op jit(solution)/shard_map/while/body/jit(_take)/select_n | solution.py:31
  165.7 14.3 %fusion.117 = f32[32,128,8,64]{1,3,2,0:T(8,128)} fusion(bf16[32,128,8,64]{1,3,2,0:T(8,128)(2,1)} %bitcast.188, bf16[32,128,8,64]{1,3,2,0:T(8,128)(2,1)} %bitcast.189, bf16[32,128,8,64]{3,2,1,0:T(8,128)(2,1)} %broadcast_select_fusion.22, f32[32,8,128]{2,1,0:T(8,128)S(1)} %get-tuple-element.638, f32[32,8,128]{2,1,0:T(8,128)S(1)} %get-tuple-element.639, ...), kind=kOutput, calls=%fused_computation.42.clone.2 | convolution fusion | flops 1094713344 | bytes 21233696 | tf_op jit(solution)/shard_map/while/body/shij,sjhd->sihd/dot_general | solution.py:106
  180.0 11.3 %fusion.118 = f32[2,128,8,64]{1,0,3,2:T(2,128)S(1)} fusion(f32[2,128,8,64]{1,0,3,2:T(2,128)S(1)} %get-tuple-element.709, f32[32,128,8,64]{1,3,2,0:T(8,128)} %fusion.117, pred[32]{0:T(512)(128)(4,1)S(1)} %get-tuple-element.640, s32[32]{0:T(128)S(1)} %slice_bitcast_fusion.8), kind=kOutput, calls=%fused_computation.43.clone.1 | convolution fusion | flops 50462848 | bytes 9437344 | tf_op jit(solution)/shard_map/while/body/sn,sihd->nihd/dot_general | solution.py:109
  214.5 198.6 %while.36 = (s32[]{:T(128)}, f32[2,128,8,64]{1,0,3,2:T(2,128)S(1)}, f32[16,128,1024]{2,1,0:T(8,128)}, s32[]{:T(128)}, s32[32,2]{0,1:T(2,128)S(1)}, /*index=5*/s3...) while((s32[]{:T(128)}, f32[2,128,8,64]{1,0,3,2:T(2,128)S(1)}, ...), condition=%wide.region_10.14_spmd, body=%wide.region_8.13_spmd.sunk | while | flops 2793639936 | bytes 384713920 | solution.py:166
  217.2 7.2 %gather_fusion.7 = bf16[32,128,1024]{2,1,0:T(8,128)(2,1)} fusion(bf16[16,128,1024]{2,1,0:T(8,128)(2,1)} %get-tuple-element.764, s32[1024]{0:T(1024)S(1)} %pad_clamp_fusion.18), kind=kCustom, calls=%fused_computation.7.clone.clone.1 | custom fusion | bytes 16777344 | tf_op jit(solution)/shard_map/while/body/jit(_take)/gather | solution.py:31
  224.4 7.5 %broadcast_select_fusion.24 = bf16[32,128,1024]{2,1,0:T(8,128)(2,1)} fusion(bf16[32,128,1024]{2,1,0:T(8,128)(2,1)} %gather_fusion.7, pred[32]{0:T(512)(128)(4,1)S(1)} %get-tuple-element.654), kind=kLoop, calls=%fused_computation.70.clone.1 | loop fusion | flops 4194304 | bytes 16777248 | tf_op jit(solution)/shard_map/while/body/jit(_take)/select_n | solution.py:31
  260.5 11.6 %broadcast_select_fusion.25 = (bf16[32,128,8,64]{3,2,1,0:T(8,128)(2,1)}, bf16[32,128,8,64]{3,2,1,0:T(8,128)(2,1)}) fusion(bf16[32,128,8,64]{3,2,1,0:T(8,128)(2,1)} %gather_fusion.8, pred[32]{0:T(512)(128)(4,1)S(1)} %get-tuple-element.657, bf16[32,128,8,64]{3,2,1,0:T(8,128)(2,1)} %gather_fusion.9), kind=kLoop, calls=%fused_computation.68.clone.1 | loop fusion | flops 4194304 | bytes 16777248 | tf_op jit(solution)/shard_map/while/body/jit(_take)/select_n | solution.py:131
  272.1 9.0 %copy.232 = bf16[32,128,8,64]{1,3,2,0:T(8,128)(2,1)} copy(bf16[32,128,8,64]{3,2,1,0:T(8,128)(2,1)} %get-tuple-element.658) | data formatting | bytes 8388608 | tf_op jit(solution)/shard_map/while/body/jit(_take)/select_n | solution.py:30
  281.1 9.0 %copy.233 = bf16[32,128,8,64]{1,3,2,0:T(8,128)(2,1)} copy(bf16[32,128,8,64]{3,2,1,0:T(8,128)(2,1)} %get-tuple-element.662) | data formatting | bytes 8388608 | tf_op jit(solution)/shard_map/while/body/jit(_take)/select_n | solution.py:131
  290.1 15.2 %select_convert_fusion.3 = bf16[32,8,128,128]{3,2,1,0:T(8,128)(2,1)S(1)} fusion(bf16[32,128,8,64]{1,3,2,0:T(8,128)(2,1)} %copy.232, bf16[32,128,8,64]{1,3,2,0:T(8,128)(2,1)} %bitcast.186, f32[32,8,128]{2,1,0:T(8,128)S(1)} %get-tuple-element.659, f32[32,8,128]{2,1,0:T(8,128)S(1)} %get-tuple-element.660, pred[32]{0:T(512)(128)(4,1)S(1)} %get-tuple-element.661), kind=kOutput, calls=%fused_computation.64.clone.1 | convolution fusion | flops 557842432 | bytes 17039392 | tf_op jit(solution)/shard_map/while/body/sihd,sjhd->shij/dot_general | solution.py:35
  305.3 8.8 %multiply_convert_fusion.2 = bf16[32,8,128,128]{3,2,1,0:T(8,128)(2,1)} fusion(bf16[32,8,128,128]{3,2,1,0:T(8,128)(2,1)S(1)} %select_convert_fusion.3, bf16[32,128,8,64]{1,3,2,0:T(8,128)(2,1)S(1)} %copy-done.2, bf16[32,128,8,64]{1,3,2,0:T(8,128)(2,1)S(1)} %bitcast.185, f32[32,8,128]{2,1,0:T(8,128)S(1)} %select_bitcast_fusion.2), kind=kOutput, calls=%fused_computation.63.clone.1 | convolution fusion | flops 553648128 | bytes 25296896 | tf_op jit(solution)/shard_map/while/body/sihd,sjhd->shij/dot_general | solution.py:135
  318.6 9.0 %copy.235 = f32[32,128,512]{2,1,0:T(8,128)} copy(f32[32,128,512]{1,2,0:T(8,128)} %bitcast.183) | data formatting | bytes 16777216 | tf_op jit(solution)/shard_map/while/body/reshape | solution.py:156
  327.6 10.2 %broadcast_multiply_fusion.2 = f32[32,8,64,128]{3,2,1,0:T(8,128)} fusion(bf16[32,128,8,64]{1,3,2,0:T(8,128)(2,1)} %copy.232, bf16[32,8,128,128]{3,2,1,0:T(8,128)(2,1)} %multiply_convert_fusion.2), kind=kOutput, calls=%fused_computation.71.clone.1 | convolution fusion | flops 538968064 | bytes 20971520 | tf_op jit(solution)/shard_map/while/body/shij,sihd->sjhd/dot_general | solution.py:147
  337.8 10.5 %multiply_bitcast_fusion.2 = f32[32,128,8,64]{1,3,2,0:T(8,128)S(1)} fusion(bf16[32,128,8,64]{1,3,2,0:T(8,128)(2,1)} %bitcast.187, bf16[32,8,128,128]{3,2,1,0:T(8,128)(2,1)} %multiply_convert_fusion.2), kind=kOutput, calls=%fused_computation.67.clone.1 | convolution fusion | flops 538968064 | bytes 20971520 | tf_op jit(solution)/shard_map/while/body/shij,sjhd->sihd/dot_general | solution.py:143
  348.3 8.4 %fusion.132 = f32[2,128,8,64]{1,0,3,2:T(2,128)S(1)} fusion(f32[2,128,8,64]{1,0,3,2:T(2,128)S(1)} %get-tuple-element.745, f32[32,128,8,64]{1,3,2,0:T(8,128)S(1)} %multiply_bitcast_fusion.2, pred[32]{0:T(512)(128)(4,1)S(1)} %get-tuple-element.661, s32[32]{0:T(128)S(1)} %get-tuple-element.665), kind=kOutput, calls=%fused_computation.72.clone.1 | convolution fusion | flops 50462848 | bytes 9437344 | tf_op jit(solution)/shard_map/while/body/sn,sihd->nihd/dot_general | solution.py:152
  356.7 9.0 %copy.236 = f32[32,128,512]{2,1,0:T(8,128)} copy(f32[32,128,512]{1,2,0:T(8,128)} %bitcast.182) | data formatting | bytes 16777216 | tf_op jit(solution)/shard_map/while/body/reshape | solution.py:156
  365.7 11.7 %pad_maximum_fusion.3 = f32[32,128,1024]{2,1,0:T(8,128)} fusion(f32[32,128,512]{2,1,0:T(8,128)} %copy.235, f32[32,128,512]{2,1,0:T(8,128)} %copy.236), kind=kLoop, calls=%fused_computation.62.clone.1 | loop fusion | flops 4194304 | bytes 33554432 | tf_op jit(solution)/shard_map/while/body/concatenate | solution.py:155
  377.4 35.5 %scatter_fusion = f32[16,128,1024]{2,1,0:T(8,128)} fusion(f32[16,128,1024]{2,1,0:T(8,128)} %get-tuple-element.746, s32[32]{0:T(128)S(1)} %get-tuple-element.666, f32[32,128,1024]{2,1,0:T(8,128)} %pad_maximum_fusion.3), kind=kCustom, calls=%fused_computation.13.clone.1 | custom fusion | flops 4194304 | bytes 50331776 | tf_op jit(solution)/shard_map/while/body/scatter-add | solution.py:159
  421.8 46.6 %reduce-scatter.12.cloned.1.call-done = bf16[256,1024]{1,0:T(8,128)(2,1)} async-done(((bf16[2048,1024]{1,0:T(8,128)(2,1)}), bf16[256,1024]{1,0:T(8,128)(2,1)}) %reduce-scatter.12.cloned.1.call-update) | async-done | bytes 524304 | tf_op jit(solution)/shard_map/reduce_scatter | solution.py:168
  478.4 22.5 %reduce-scatter.16.cloned.1.call-done = bf16[128,512]{1,0:T(8,128)(2,1)} async-done(((bf16[1024,512]{1,0:T(8,128)(2,1)}), bf16[128,512]{1,0:T(8,128)(2,1)}) %reduce-scatter.16.cloned.1.call-update) | async-done | bytes 131088
  502.8 13.8 %reduce-scatter.14.cloned.1.call-done = bf16[256,512]{1,0:T(8,128)(2,1)} async-done(((bf16[256,1024]{1,0:T(8,128)(2,1)}), bf16[256,512]{1,0:T(8,128)(2,1)}) %reduce-scatter.14.cloned.1.call-update) | async-done | bytes 262160 | tf_op jit(solution)/shard_map/reduce_scatter | solution.py:184
  518.5 32.6 %reduce-scatter.18.cloned.1.call-done = bf16[128,512]{1,0:T(8,128)(2,1)} async-done(((bf16[1024,512]{1,0:T(8,128)(2,1)}), bf16[128,512]{1,0:T(8,128)(2,1)}) %reduce-scatter.18.cloned.1.call-update) | async-done | bytes 131088
  552.9 31.2 %reduce-scatter.20.cloned.1.call-done = bf16[128,512]{1,0:T(8,128)(2,1)} async-done(((bf16[1024,512]{1,0:T(8,128)(2,1)}), bf16[128,512]{1,0:T(8,128)(2,1)}) %reduce-scatter.20.cloned.1.call-update) | async-done | bytes 131088
  (117 shorter events, 119.4 us)
Async XLA Ops:
  7.2 6.6 %copy-start = (bf16[1024,512]{1,0:T(8,128)(2,1)S(1)}, bf16[1024,512]{1,0:T(8,128)(2,1)}, u32[]{:S(2)}) copy-start(bf16[1024,512]{1,0:T(8,128)(2,1)} %param.20) | copy-start | bytes 3145732
  7.2 54.7 %copy-start.9 = (s32[1,32,2]{1,2,0:T(2,128)S(1)}, s32[1,32,2]{1,2,0:T(2,128)}, u32[]{:S(2)}) copy-start(s32[1,32,2]{1,2,0:T(2,128)} %param.24) | copy-start | bytes 772
  7.2 54.7 %all-gather.2.cloned.1.call-start = ((), (), s32[]{:S(2)}) async-start(), calls=%async_computation.5 | async-start | bytes 4718592 | tf_op jit(solution)/shard_map/all_gather | solution.py:70
  11.9 456.5 %reduce-scatter.12.cloned.1.call-start = ((), (), s32[]{:S(2)}) async-start(), calls=%async_computation.6 | async-start | bytes 4718592 | tf_op jit(solution)/shard_map/reduce_scatter | solution.py:168
  13.7 48.1 %copy-start.5 = (bf16[2,128,8,64]{1,0,3,2:T(2,128)(2,1)}, bf16[2,128,8,64]{1,0,3,2:T(2,128)(2,1)S(1)}, u32[]{:S(2)}) copy-start(bf16[2,128,8,64]{1,0,3,2:T(2,128)(2,1)S(1)} %reshape.142) | copy-start | bytes 786436
  117.5 91.5 %copy-start.6 = (bf16[2,128,8,64]{1,0,3,2:T(2,128)(2,1)S(1)}, bf16[2,128,8,64]{1,0,3,2:T(2,128)(2,1)}, u32[]{:S(2)}) copy-start(bf16[2,128,8,64]{1,0,3,2:T(2,128)(2,1)} %copy-done.5) | copy-start | bytes 786436
  209.0 5.5 copy-start.1
  214.5 0.7 copy-start.10
  290.1 15.2 %copy-start.2 = (bf16[32,128,8,64]{1,3,2,0:T(8,128)(2,1)S(1)}, bf16[32,128,8,64]{1,3,2,0:T(8,128)(2,1)}, u32[]{:S(2)}) copy-start(bf16[32,128,8,64]{1,3,2,0:T(8,128)(2,1)} %copy.233) | copy-start | bytes 12582916 | tf_op jit(solution)/shard_map/while
  290.1 15.2 %copy-start.3 = (bf16[32,128,512]{1,2,0:T(8,128)(2,1)S(1)}, bf16[32,128,512]{1,2,0:T(8,128)(2,1)}, u32[]{:S(2)}) copy-start(bf16[32,128,512]{1,2,0:T(8,128)(2,1)} %copy.234) | copy-start | bytes 12582916 | tf_op jit(solution)/shard_map/while
  377.4 35.5 %copy-start.11 = (s32[32,2]{0,1:T(2,128)S(1)}, s32[32,2]{0,1:T(2,128)}, u32[]{:S(2)}) copy-start(s32[32,2]{0,1:T(2,128)} %copy-done.10) | copy-start | bytes 772 | tf_op jit(solution)/shard_map/while
  413.1 6.3 %copy-start.4 = (bf16[256,1024]{1,0:T(8,128)(2,1)S(1)}, bf16[256,1024]{1,0:T(8,128)(2,1)}, u32[]{:S(2)}) copy-start(bf16[256,1024]{1,0:T(8,128)(2,1)} %param.19) | copy-start | bytes 1572868
  419.2 81.8 %reduce-scatter.16.cloned.1.call-start = ((), (), s32[]{:S(2)}) async-start(), calls=%async_computation.8 | async-start | bytes 1179648
  421.2 95.4 %reduce-scatter.14.cloned.1.call-start = ((), (), s32[]{:S(2)}) async-start(), calls=%async_computation.7 | async-start | bytes 786432 | tf_op jit(solution)/shard_map/reduce_scatter | solution.py:184
  421.8 55.7 %copy-start.8 = (bf16[2,128,8,64]{1,0,3,2:T(2,128)(2,1)S(1)}, bf16[2,128,8,64]{1,0,3,2:T(2,128)(2,1)}, u32[]{:S(2)}) copy-start(bf16[2,128,8,64]{1,0,3,2:T(2,128)(2,1)} %get-tuple-element.426) | copy-start | bytes 786436
  468.4 7.3 %copy-start.7 = (bf16[256,1024]{1,0:T(8,128)(2,1)S(1)}, bf16[256,1024]{1,0:T(8,128)(2,1)}, u32[]{:S(2)}) copy-start(bf16[256,1024]{1,0:T(8,128)(2,1)} %reduce-scatter.12.cloned.1.call-done) | copy-start | bytes 1572868
  472.8 78.2 %reduce-scatter.18.cloned.1.call-start = ((), (), s32[]{:S(2)}) async-start(), calls=%async_computation.9 | async-start | bytes 1179648
  475.6 108.5 %reduce-scatter.20.cloned.1.call-start = ((), (), s32[]{:S(2)}) async-start(), calls=%async_computation.10 | async-start | bytes 1179648
Sparse Core Ops, SparseCore 0:
  12.0 49.8 all-gather.1
  419.3 49.0 reduce-scatter.11
  470.7 30.2 reduce-scatter.15
  503.6 12.9 reduce-scatter.13
  518.9 32.0 reduce-scatter.17
  553.2 30.8 reduce-scatter.19
where the time goes:
time: 605 us; the launch traced here: 593 us
  waiting for transfers between devices  192 us (32%)
  local copies, waits for them, and re-layouts  142 us (23%)
  other arithmetic  116 us (19%)
  matrix products  108 us (18%)
  loops' own time  18.5 us (3%)
  between operations  15.4 us (3%)
    unnamed x9, waiting for transfers between devices  86.4 us
    reduce_scatter x1, waiting for transfers between devices, per_device(): lax.psum_scatter(key_grads.astype(jnp.bfloat16), 'col', scatter_dimension...  46.6 us
    all_gather x1, waiting for transfers between devices, per_device(): key_table = lax.all_gather(local_table, 'col', axis=0, tiled=True)  45.1 us
    scatter-add x1, other arithmetic, backward_turn(): jax.ops.segment_sum(rows_update, key_block, num_segments=key_blocks_all)  35.5 us
    dot_general x2, matrix products, batch_tiles(): jnp.einsum('sihd,sjhd->shij', query_pick, key_pick, preferred_element_typ...  27.4 us
    slice x4, local copies, waits for them, and re-layouts, batch_tiles(): key_pick = table_pick[:, :, :head_cols].reshape(width, BLK, head_count, DH)  25.2 us
    gather x3, local copies, waits for them, and re-layouts, batch_tiles(): table_pick = jnp.take(table_tiles, key_block, axis=0)  21.6 us
    select_n x3, other arithmetic, batch_tiles(): table_pick = jnp.take(table_tiles, key_block, axis=0)  19.5 us
  transfers between devices with their start and end apart: 6, of which 6 were waited for; matrix products, arithmetic and copies ran while one was open for 4% of the time, Pallas kernels for 0%

commit v1 on v0

--- a/solution.py
+++ b/solution.py
@@ -1,8 +1,11 @@
+import functools
 import math
 
 import jax
 import jax.numpy as jnp
 from jax import lax
+from jax.experimental import pallas as pl
+from jax.experimental.pallas import tpu as pltpu
 from jax.sharding import PartitionSpec as P
 
 DH = 64
@@ -45,7 +48,7 @@
     return jnp.where(slot_live[:, None, None, None], weights, 0.0).astype(jnp.bfloat16)
 
 
-def per_device(
+def per_device_slots(
     node_states, query_weight, key_weight, value_weight, output_grad, pair_list, pair_count
 ):
     head_cols = query_weight.shape[1]
@@ -208,9 +211,400 @@
     return (attended, node_grad, query_grad, key_grad, value_grad)
 
 
+MESH = pl.DeviceIdType.MESH
+GROUP = 4
+
+
+def meet(axes):
+    barrier = pltpu.get_barrier_semaphore()
+    total = 0
+    for axis, count in axes:
+        me = lax.axis_index(axis)
+        for step in range(1, count):
+            peer = lax.rem(me + step, count)
+            pl.semaphore_signal(barrier, inc=1, device_id={axis: peer}, device_id_type=MESH)
+            total += 1
+    pl.semaphore_wait(barrier, total)
+
+
+def spread_kernel(
+    n, x_ref, wq_ref, wk_ref, wv_ref, grad_ref, code_ref, heads_ref, codes_ref,
+    outbox, own_sem, send_sem, recv_sem, code_send, code_recv, code_own,
+):
+    me = lax.axis_index("col")
+    meet([("col", n)])
+
+    def code_copy(peer, slot):
+        return pltpu.make_async_remote_copy(
+            src_ref=code_ref, dst_ref=codes_ref.at[slot], send_sem=code_send.at[peer],
+            recv_sem=code_recv.at[slot], device_id={"col": peer}, device_id_type=MESH,
+        )
+
+    def head_copy(peer, slot):
+        return pltpu.make_async_remote_copy(
+            src_ref=outbox.at[peer], dst_ref=heads_ref.at[slot], send_sem=send_sem.at[peer],
+            recv_sem=recv_sem.at[slot], device_id={"col": peer}, device_id_type=MESH,
+        )
+
+    peers = [lax.rem(me + step, n) for step in range(1, n)]
+    for peer in peers:
+        code_copy(peer, me).start()
+    own_code = pltpu.make_async_copy(code_ref, codes_ref.at[me], code_own)
+    own_code.start()
+    x = x_ref[...]
+    factor = 1.0 / math.sqrt(DH)
+    queries = jnp.dot(x, wq_ref[...], preferred_element_type=jnp.float32)
+    queries = (queries.astype(jnp.bfloat16).astype(jnp.float32) * factor).astype(jnp.bfloat16)
+    keys = jnp.dot(x, wk_ref[...], preferred_element_type=jnp.float32).astype(jnp.bfloat16)
+    values = jnp.dot(x, wv_ref[...], preferred_element_type=jnp.float32).astype(jnp.bfloat16)
+    grads = grad_ref[...]
+    for head in range(n):
+        cols = slice(head * DH, (head + 1) * DH)
+        outbox[head] = jnp.concatenate(
+            [queries[:, cols], grads[:, cols], keys[:, cols], values[:, cols]], axis=1
+        )
+    for peer in peers:
+        head_copy(peer, me).start()
+    own = pltpu.make_async_copy(outbox.at[me], heads_ref.at[me], own_sem)
+    own.start()
+    own.wait()
+    own_code.wait()
+    for peer in peers:
+        code_copy(peer, peer).wait_recv()
+        head_copy(peer, peer).wait_recv()
+    for peer in peers:
+        code_copy(peer, me).wait_send()
+        head_copy(peer, me).wait_send()
+
+
+def spread(node_states, query_weight, key_weight, value_weight, output_grad, codes, n):
+    rows = node_states.shape[0]
+    width = 4 * DH
+    vmem = pl.BlockSpec(memory_space=pltpu.VMEM)
+    return pl.pallas_call(
+        functools.partial(spread_kernel, n),
+        out_shape=(
+            jax.ShapeDtypeStruct((n, rows, width), jnp.bfloat16),
+            jax.ShapeDtypeStruct((n,) + codes.shape, jnp.int32),
+        ),
+        in_specs=[vmem] * 6,
+        out_specs=(pl.BlockSpec(memory_space=pl.ANY), pl.BlockSpec(memory_space=pl.ANY)),
+        scratch_shapes=[
+            pltpu.VMEM((n, rows, width), jnp.bfloat16),
+            pltpu.SemaphoreType.DMA,
+            pltpu.SemaphoreType.DMA((n,)),
+            pltpu.SemaphoreType.DMA((n,)),
+            pltpu.SemaphoreType.DMA((n,)),
+            pltpu.SemaphoreType.DMA((n,)),
+            pltpu.SemaphoreType.DMA,
+        ],
+        compiler_params=pltpu.CompilerParams(
+            collective_id=0, has_side_effects=True, vmem_limit_bytes=24 << 20
+        ),
+        cost_estimate=pl.CostEstimate(
+            flops=6 * rows * node_states.shape[1] * n * DH, bytes_accessed=40 << 20, transcendentals=0
+        ),
+        name="spread_heads",
+    )(node_states, query_weight, key_weight, value_weight, output_grad, codes)
+
+
+def attend_kernel(
+    n, blocks, codes_ref, heads_ref, out_ref, pairs_acc, scores_buf, grads_buf, found, counts
+):
+    lanes = lax.broadcasted_iota(jnp.int32, (BLK, 2 * DH), 1)
+    first = lanes < DH
+    key_total = n * blocks
+    nt = (((1,), (1,)), ((), ()))
+    pairs_acc[...] = jnp.zeros_like(pairs_acc)
+
+    def collect(panel):
+        for q in range(blocks):
+            counts[q] = 0
+            for k in range(key_total):
+                found[q, k] = 0
+        total = codes_ref[panel, 2, 0]
+
+        def one(slot, carry):
+            q = codes_ref[panel, 0, slot]
+            place = counts[q]
+            found[q, place] = codes_ref[panel, 1, slot]
+            counts[q] = place + 1
+            return carry
+
+        lax.fori_loop(0, total, one, 0)
+
+    def work(panel, groups):
+        width = GROUP * BLK
+        stacks = []
+        for q in range(blocks):
+            both = heads_ref[panel, q * BLK : (q + 1) * BLK, : 2 * DH]
+            zero = jnp.zeros_like(both)
+            stacks.append(
+                jnp.concatenate([jnp.where(first, both, zero), jnp.where(first, zero, both)], axis=0)
+            )
+
+        def table(q, g):
+            parts = []
+            for j in range(GROUP):
+                k = found[q, g * GROUP + j]
+                start = pl.multiple_of(lax.rem(k, blocks) * BLK, BLK)
+                parts.append(heads_ref[lax.div(k, blocks), pl.ds(start, BLK), 2 * DH :])
+            return jnp.concatenate(parts, axis=0)
+
+        tops, totals, outs, deltas = [], [], [], []
+        for q in range(blocks):
+            top = jnp.full((BLK, BLK), LOWEST, jnp.float32)
+            for g in range(groups):
+                both = lax.dot_general(stacks[q], table(q, g), nt, preferred_element_type=jnp.float32)
+                grads_buf[q, g] = both[BLK:]
+                for j in range(GROUP):
+                    tile = both[:BLK, j * BLK : (j + 1) * BLK]
+                    live = g * GROUP + j < counts[q]
+                    tile = jnp.where(live, tile, LOWEST)
+                    scores_buf[q, g, :, j * BLK : (j + 1) * BLK] = tile
+                    top = jnp.maximum(top, tile)
+            tops.append(jnp.max(top, axis=1, keepdims=True))
+        for q in range(blocks):
+            total = jnp.zeros((BLK, BLK), jnp.float32)
+            for g in range(groups):
+                terms = jnp.exp(scores_buf[q, g] - tops[q])
+                scores_buf[q, g] = terms
+                for j in range(GROUP):
+                    total = total + terms[:, j * BLK : (j + 1) * BLK]
+            totals.append(1.0 / jnp.sum(total, axis=1, keepdims=True))
+        for q in range(blocks):
+            out = jnp.zeros((BLK, 2 * DH), jnp.float32)
+            for g in range(groups):
+                weights = (scores_buf[q, g] * totals[q]).astype(jnp.bfloat16)
+                out = out + jnp.dot(weights, table(q, g), preferred_element_type=jnp.float32)
+            outs.append(out)
+            grad = stacks[q][BLK:].astype(jnp.float32)
+            deltas.append(jnp.sum(grad * out, axis=1, keepdims=True))
+        for q in range(blocks):
+            rows_grad = jnp.zeros((BLK, 2 * DH), jnp.float32)
+            turned = stacks[q].T
+            for g in range(groups):
+                weights = (scores_buf[q, g] * totals[q]).astype(jnp.bfloat16)
+                score_grad = (
+                    weights.astype(jnp.float32) * (grads_buf[q, g] - deltas[q])
+                ).astype(jnp.bfloat16)
+                rows_grad = rows_grad + jnp.dot(
+                    score_grad, table(q, g), preferred_element_type=jnp.float32
+                )
+                pair = jnp.dot(
+                    turned,
+                    jnp.concatenate([score_grad, weights], axis=0),
+                    preferred_element_type=jnp.float32,
+                )
+                for j in range(GROUP):
+                    k = found[q, g * GROUP + j]
+                    pairs_acc[k] = pairs_acc[k] + pair[:, j * BLK : (j + 1) * BLK]
+            factor = 1.0 / math.sqrt(DH)
+            out_ref[panel, q * BLK : (q + 1) * BLK, : 2 * DH] = jnp.where(
+                first, rows_grad * factor, outs[q]
+            ).astype(jnp.bfloat16)
+
+    def one_panel(panel, carry):
+        collect(panel)
+        most = counts[0]
+        for q in range(1, blocks):
+            most = jnp.maximum(most, counts[q])
+        groups = lax.div(most + (GROUP - 1), GROUP)
+        for size in range(1, key_total // GROUP + 1):
+            pl.when(groups == size)(functools.partial(work, panel, size))
+        return carry
+
+    lax.fori_loop(0, n, one_panel, 0)
+    for k in range(key_total):
+        row = (k % blocks) * BLK
+        out_ref[k // blocks, row : row + BLK, 2 * DH :] = pairs_acc[k].T.astype(jnp.bfloat16)
+
+
+def attend(heads, codes, n, blocks):
+    key_total = n * blocks
+    groups = key_total // GROUP
+    tiles = key_total * key_total
+    return pl.pallas_call(
+        functools.partial(attend_kernel, n, blocks),
+        out_shape=jax.ShapeDtypeStruct(heads.shape, jnp.bfloat16),
+        in_specs=[
+            pl.BlockSpec(memory_space=pltpu.SMEM),
+            pl.BlockSpec(memory_space=pltpu.VMEM),
+        ],
+        out_specs=pl.BlockSpec(memory_space=pltpu.VMEM),
+        scratch_shapes=[
+            pltpu.VMEM((key_total, 2 * DH, BLK), jnp.float32),
+            pltpu.VMEM((blocks, groups, BLK, GROUP * BLK), jnp.float32),
+            pltpu.VMEM((blocks, groups, BLK, GROUP * BLK), jnp.float32),
+            pltpu.SMEM((blocks, key_total), jnp.int32),
+            pltpu.SMEM((blocks,), jnp.int32),
+        ],
+        compiler_params=pltpu.CompilerParams(vmem_limit_bytes=24 << 20),
+        cost_estimate=pl.CostEstimate(
+            flops=tiles * 24 * BLK * BLK * DH, bytes_accessed=80 << 20,
+            transcendentals=tiles * BLK * BLK,
+        ),
+        name="attend_heads",
+    )(codes, heads)
+
+
+def collect_kernel(
+    n, n_row, res_ref, x_ref, wq_ref, wk_ref, wv_ref,
+    att_ref, node_ref, qg_ref, kg_ref, vg_ref,
+    inbox, terms_out, terms_in, part_out, part_in,
+    send_sem, recv_sem, term_send, term_recv, row_send, row_recv,
+):
+    me = lax.axis_index("col")
+    my_row = lax.axis_index("row")
+    meet([("col", n), ("row", n_row)])
+    peers = [lax.rem(me + step, n) for step in range(1, n)]
+    row_peers = [lax.rem(my_row + step, n_row) for step in range(1, n_row)]
+    cols = part_out.shape[2]
+
+    def res_copy(peer, slot):
+        return pltpu.make_async_remote_copy(
+            src_ref=res_ref.at[peer], dst_ref=inbox.at[slot], send_sem=send_sem.at[peer],
+            recv_sem=recv_sem.at[slot], device_id={"col": peer}, device_id_type=MESH,
+        )
+
+    def term_copy(peer, slot):
+        return pltpu.make_async_remote_copy(
+            src_ref=terms_out.at[peer], dst_ref=terms_in.at[slot], send_sem=term_send.at[peer],
+            recv_sem=term_recv.at[slot], device_id={"col": peer}, device_id_type=MESH,
+        )
+
+    def row_copy(peer, slot):
+        return pltpu.make_async_remote_copy(
+            src_ref=part_out.at[peer], dst_ref=part_in.at[slot], send_sem=row_send.at[peer],
+            recv_sem=row_recv.at[slot], device_id={"row": peer}, device_id_type=MESH,
+        )
+
+    for peer in peers:
+        res_copy(peer, me).start()
+    inbox[me] = res_ref[me]
+    rows = res_ref.shape[1]
+    chunk = x_ref.shape[1] // n
+    turned = res_ref[...].reshape(n * rows, 4 * DH).T
+    for peer in range(n):
+        term = jnp.dot(
+            turned, x_ref[:, peer * chunk : (peer + 1) * chunk], preferred_element_type=jnp.float32
+        ).astype(jnp.bfloat16)
+        terms_out[peer, :DH] = term[:DH]
+        terms_out[peer, DH:] = term[2 * DH :]
+    for peer in peers:
+        term_copy(peer, me).start()
+    terms_in[me] = terms_out[me]
+    for peer in peers:
+        res_copy(peer, peer).wait_recv()
+
+    def piece(which):
+        return jnp.concatenate(
+            [inbox[h, :, which * DH : (which + 1) * DH] for h in range(n)], axis=1
+        )
+
+    nt = (((1,), (1,)), ((), ()))
+    grads = [piece(0), piece(2), piece(3)]
+    weights = [wq_ref, wk_ref, wv_ref]
+    for r in range(n_row):
+        span = slice(r * cols, (r + 1) * cols)
+        part = jnp.zeros((rows, cols), jnp.float32)
+        for grad, weight in zip(grads, weights):
+            part = part + lax.dot_general(
+                grad, weight[span, :], nt, preferred_element_type=jnp.float32
+            )
+        part_out[r] = part.astype(jnp.bfloat16)
+    for peer in row_peers:
+        row_copy(peer, my_row).start()
+    att_ref[...] = piece(1)
+    for peer in peers:
+        term_copy(peer, peer).wait_recv()
+    for which, ref in enumerate((qg_ref, kg_ref, vg_ref)):
+        for h in range(0, n, 2):
+            pair = jnp.concatenate(
+                [
+                    terms_in[h, which * DH : (which + 1) * DH],
+                    terms_in[h + 1, which * DH : (which + 1) * DH],
+                ],
+                axis=0,
+            )
+            ref[:, h * DH : (h + 2) * DH] = pair.astype(jnp.float32).T
+    total = part_out[my_row].astype(jnp.float32)
+    for peer in row_peers:
+        row_copy(peer, peer).wait_recv()
+        total = total + part_in[peer].astype(jnp.float32)
+    node_ref[...] = total
+    for peer in peers:
+        res_copy(peer, me).wait_send()
+        term_copy(peer, me).wait_send()
+    for peer in row_peers:
+        row_copy(peer, my_row).wait_send()
+
+
+def collect_grads(res, x_all, query_weight, key_weight, value_weight, n, n_row):
+    rows = res.shape[1]
+    depth = x_all.shape[1]
+    cols = depth // n_row
+    chunk = depth // n
+    head_cols = n * DH
+    vmem = pl.BlockSpec(memory_space=pltpu.VMEM)
+    dma = pltpu.SemaphoreType.DMA
+    return pl.pallas_call(
+        functools.partial(collect_kernel, n, n_row),
+        out_shape=(
+            jax.ShapeDtypeStruct((rows, head_cols), jnp.bfloat16),
+            jax.ShapeDtypeStruct((rows, cols), jnp.float32),
+            jax.ShapeDtypeStruct((chunk, head_cols), jnp.float32),
+            jax.ShapeDtypeStruct((chunk, head_cols), jnp.float32),
+            jax.ShapeDtypeStruct((chunk, head_cols), jnp.float32),
+        ),
+        in_specs=[vmem] * 5,
+        out_specs=(vmem,) * 5,
+        scratch_shapes=[
+            pltpu.VMEM(res.shape, jnp.bfloat16),
+            pltpu.VMEM((n, 3 * DH, chunk), jnp.bfloat16),
+            pltpu.VMEM((n, 3 * DH, chunk), jnp.bfloat16),
+            pltpu.VMEM((n_row, rows, cols), jnp.bfloat16),
+            pltpu.VMEM((n_row, rows, cols), jnp.bfloat16),
+            dma((n,)), dma((n,)), dma((n,)), dma((n,)), dma((n_row,)), dma((n_row,)),
+        ],
+        compiler_params=pltpu.CompilerParams(
+            collective_id=1, has_side_effects=True, vmem_limit_bytes=40 << 20
+        ),
+        name="collect_grads",
+    )(res, x_all, query_weight, key_weight, value_weight)
+
+
+def per_device_heads(
+    n, n_row, node_states, query_weight, key_weight, value_weight, output_grad, pair_list, pair_count
+):
+    blocks = node_states.shape[0] // BLK
+    slots = pair_list.shape[1]
+    listed = jnp.pad(pair_list[0].T, ((0, 0), (0, BLK - slots)))
+    total = jnp.broadcast_to(pair_count[0], (6, BLK))
+    codes = jnp.concatenate([listed, total], axis=0)
+    x_all = lax.all_gather(node_states, "col", axis=0, tiled=True)
+    heads, codes_all = spread(
+        node_states, query_weight, key_weight, value_weight, output_grad, codes, n
+    )
+    res = attend(heads, codes_all, n, blocks)
+    return collect_grads(res, x_all, query_weight, key_weight, value_weight, n, n_row)
+
+
+def per_device(mesh, *arrays):
+    n, n_row = mesh.shape["col"], mesh.shape["row"]
+    node_states, query_weight, pair_list = arrays[0], arrays[1], arrays[5]
+    blocks = node_states.shape[0] // BLK
+    one_head_each = query_weight.shape[1] == n * DH and n % 2 == 0
+    tiled = (n * blocks) % GROUP == 0 and pair_list.shape[1] <= BLK
+    lanes = node_states.shape[1] % (n * BLK) == 0 and node_states.shape[1] % (n_row * BLK) == 0
+    if one_head_each and tiled and lanes:
+        return per_device_heads(n, n_row, *arrays)
+    return per_device_slots(*arrays)
+
+
 def solution(mesh):
     return jax.shard_map(
-        per_device,
+        functools.partial(per_device, mesh),
         mesh=mesh,
         in_specs=(
             P(("groups", "col"), None),

time: 605 us -> 140 us (0.23)
  the two profiles are of different devices: /device:TPU:0 before, /device:TPU:25 now
where the time goes in v1:
time: 140 us; the launch traced here: 141 us
  Pallas kernels  111 us (79%)
  between operations  14.7 us (10%)
  local copies, waits for them, and re-layouts  13.7 us (10%)
    pallas_call x1, Pallas kernels, spread(): pl.pallas_call(functools.partial(spread_kernel, n), out_shape=(jax.ShapeD...  56.6 us
    pallas_call x1, Pallas kernels, collect_grads(): pl.pallas_call(functools.partial(collect_kernel, n, n_row), out_shape=(ja...  37.7 us
    pallas_call x1, Pallas kernels, attend(): pl.pallas_call(functools.partial(attend_kernel, n, blocks), out_shape=jax...  16.4 us
    unnamed x27, local copies, waits for them, and re-layouts  13.7 us
  transfers between devices with their start and end apart: 1, of which 0 were waited for; matrix products, arithmetic and copies ran while one was open for 0% of the time, Pallas kernels for 52%

profile of v1, /device:TPU:25, one launch (start us, length us, event | category | flops | bytes accessed | tf_op | source)
XLA Modules:
  0.0 140.6 jit_solution(14109350430821317276)
XLA Ops:
  7.2 0.0 all-gather.2.cloned.1.call-start
  7.2 0.7 all-gather.2.cloned.1.call-update
  8.5 0.7 pad_select_fusion.code_ref
  9.2 0.0 copy-start.1
  9.2 1.2 copy-done.1
  10.5 0.0 copy-start.3
  10.5 1.2 copy-done.3
  11.7 0.0 copy-start.5
  11.7 1.2 copy-done.5
  12.9 0.0 copy-start.7
  12.9 1.0 copy-done.7
  13.9 0.0 copy-start.10
  13.9 0.9 copy-done.10
  14.9 56.6 %spread_heads.1 = (bf16[8,256,256]{2,1,0:T(8,128)(2,1)S(1)}, s32[8,8,128]{2,1,0:T(8,128)S(1)}) custom-call(bf16[256,1024]{1,0:T(8,128)(2,1)S(1)} %copy-done.7, bf16[1024,512]{1,0:T(8,128)(2,1)S(1)} %copy-done.1, bf16[1024,512]{1,0:T(8,128)(2,1)S(1)} %copy-done.3, bf16[1024,512]{1,0:T(8,128)(2,1)S(1)} %copy-done.5, bf16[256,512]{1,0:T(8,128)(2,1)S(1)} %copy-done.10, ...), custom_call_target="tpu_custom_call" | custom-call | flops 805306368 | bytes 41943040 | tf_op jit(solution)/shard_map/spread_heads/pallas_call | solution.py:284
  71.5 0.0 copy-start.2
  71.5 0.0 copy-start.4
  71.6 0.0 copy-start.6
  71.6 16.4 %attend_heads.1.res_ref = bf16[8,256,256]{2,1,0:T(8,128)(2,1)S(1)} custom-call(s32[8,8,128]{2,1,0:T(8,128)S(1)} %get-tuple-element.7.codes_ref, bf16[8,256,256]{2,1,0:T(8,128)(2,1)S(1)} %get-tuple-element.8.heads_ref), custom_call_target="tpu_custom_call" | custom-call | flops 6442450944 | bytes 83886080 | tf_op jit(solution)/shard_map/attend_heads/pallas_call | solution.py:427
  88.0 0.0 copy-start.8
  88.0 1.0 copy-done.8
  89.0 0.0 copy-done.2
  89.0 0.0 copy-done.4
  89.0 0.0 copy-done.6
  89.0 0.0 copy-start
  89.0 2.2 %copy-done = bf16[2048,1024]{1,0:T(8,128)(2,1)S(1)} copy-done((bf16[2048,1024]{1,0:T(8,128)(2,1)S(1)}, bf16[2048,1024]{1,0:T(8,128)(2,1)}, u32[]{:S(2)}) %copy-start) | copy-done | bytes 4194328
  91.2 1.2 copy-done.9
  92.4 37.7 %collect_grads.1 = (bf16[256,512]{1,0:T(8,128)(2,1)S(1)}, f32[256,512]{1,0:T(8,128)S(1)}, f32[128,512]{1,0:T(8,128)S(1)}, f32[128,512]{1,0:T(8,128)S(1)}, f32[128,512]{1,0:T(8,128)S(1)}) custom-call(bf16[8,256,256]{2,1,0:T(8,128)(2,1)S(1)} %copy-done.9, bf16[2048,1024]{1,0:T(8,128)(2,1)S(1)} %copy-done, bf16[1024,512]{1,0:T(8,128)(2,1)S(1)} %copy-done.2, ...), custom_call_target="tpu_custom_call" | custom-call | tf_op jit(solution)/shard_map/collect_grads/pallas_call | solution.py:551
  130.2 0.7 copy.18
  130.9 0.8 copy.19
  131.6 0.7 copy.20
  132.4 0.7 copy.21
  133.1 0.7 copy.22
  (2 shorter events, 0.0 us)
Async XLA Ops:
  7.2 81.8 %all-gather.2.cloned.1.call-start = ((), (), s32[]{:S(2)}) async-start(), calls=%async_computation | async-start | bytes 4718592 | tf_op jit(solution)/shard_map/all_gather | solution.py:585
  9.2 1.2 copy-start.1
  10.5 1.2 copy-start.3
  11.7 1.2 copy-start.5
  12.9 1.0 copy-start.7
  13.9 0.9 copy-start.10
  71.5 17.4 %copy-start.2 = (bf16[1024,512]{1,0:T(8,128)(2,1)S(1)}, bf16[1024,512]{1,0:T(8,128)(2,1)}, u32[]{:S(2)}) copy-start(bf16[1024,512]{1,0:T(8,128)(2,1)} %wq_ref.3) | copy-start | bytes 3145732
  71.5 17.4 %copy-start.4 = (bf16[1024,512]{1,0:T(8,128)(2,1)S(1)}, bf16[1024,512]{1,0:T(8,128)(2,1)}, u32[]{:S(2)}) copy-start(bf16[1024,512]{1,0:T(8,128)(2,1)} %wk_ref.3) | copy-start | bytes 3145732
  71.6 17.4 %copy-start.6 = (bf16[1024,512]{1,0:T(8,128)(2,1)S(1)}, bf16[1024,512]{1,0:T(8,128)(2,1)}, u32[]{:S(2)}) copy-start(bf16[1024,512]{1,0:T(8,128)(2,1)} %wv_ref.3) | copy-start | bytes 3145732
  88.0 1.0 copy-start.8
  89.0 2.2 %copy-start = (bf16[2048,1024]{1,0:T(8,128)(2,1)S(1)}, bf16[2048,1024]{1,0:T(8,128)(2,1)}, u32[]{:S(2)}) copy-start(bf16[2048,1024]{1,0:T(8,128)(2,1)} %all-gather.2.cloned.1.call-done.x_ref) | copy-start | bytes 12582916
  91.2 1.2 copy-start.9
Sparse Core Ops, SparseCore 0:
  9.6 68.7 all-gather.1

commit v2 on v1

--- a/solution.py
+++ b/solution.py
@@ -228,11 +228,32 @@
 
 
 def spread_kernel(
-    n, x_ref, wq_ref, wk_ref, wv_ref, grad_ref, code_ref, heads_ref, codes_ref,
-    outbox, own_sem, send_sem, recv_sem, code_send, code_recv, code_own,
+    n, x_ref, wq_ref, wk_ref, wv_ref, grad_ref, code_ref, heads_ref, codes_ref, x_all,
+    grads, weights, outbox, inbox, own_sem, load_sem, grad_send, grad_recv, code_send, code_recv,
+    chain_send, chain_recv, core_send, core_recv, row_send, row_recv,
 ):
     me = lax.axis_index("col")
-    meet([("col", n)])
+    half = lax.axis_index("row")
+    other = 1 - half
+    near = n // 2
+    z = lax.div(me, 2)
+    k = lax.rem(me, 2)
+    twin = 2 * z + 1 - k
+
+    loads = [
+        pltpu.make_async_copy(
+            ref.at[:, pl.ds(pl.multiple_of(z * 2 * DH, 2 * DH), 2 * DH)],
+            weights.at[i],
+            load_sem.at[i],
+        )
+        for i, ref in enumerate((wq_ref, wk_ref, wv_ref))
+    ]
+    loads.append(pltpu.make_async_copy(grad_ref, grads, load_sem.at[3]))
+    loads.append(pltpu.make_async_copy(x_ref, x_all.at[me], load_sem.at[4]))
+    loads.append(pltpu.make_async_copy(code_ref, codes_ref.at[me], load_sem.at[5]))
+    for load in loads:
+        load.start()
+    meet([("col", n), ("row", 2)])
 
     def code_copy(peer, slot):
         return pltpu.make_async_remote_copy(
@@ -240,72 +261,172 @@
             recv_sem=code_recv.at[slot], device_id={"col": peer}, device_id_type=MESH,
         )
 
-    def head_copy(peer, slot):
+    def grad_copy(peer, slot):
         return pltpu.make_async_remote_copy(
-            src_ref=outbox.at[peer], dst_ref=heads_ref.at[slot], send_sem=send_sem.at[peer],
-            recv_sem=recv_sem.at[slot], device_id={"col": peer}, device_id_type=MESH,
+            src_ref=outbox.at[peer], dst_ref=inbox.at[slot], send_sem=grad_send.at[peer],
+            recv_sem=grad_recv.at[slot], device_id={"col": peer}, device_id_type=MESH,
+        )
+
+    def chain_copy(src, origin, side, target):
+        return pltpu.make_async_remote_copy(
+            src_ref=src, dst_ref=x_all.at[2 * origin + k, half],
+            send_sem=chain_send.at[side, origin], recv_sem=chain_recv.at[origin],
+            device_id={"col": 2 * target + k}, device_id_type=MESH,
+        )
+
+    def core_copy(src, origin, part, core):
+        return pltpu.make_async_remote_copy(
+            src_ref=src, dst_ref=x_all.at[2 * origin + core, part],
+            send_sem=core_send.at[origin, part], recv_sem=core_recv.at[origin, part],
+            device_id={"col": twin}, device_id_type=MESH,
+        )
+
+    def row_copy(src, origin, part):
+        return pltpu.make_async_remote_copy(
+            src_ref=src, dst_ref=x_all.at[2 * origin + k, part],
+            send_sem=row_send.at[origin], recv_sem=row_recv.at[origin],
+            device_id={"row": other}, device_id_type=MESH,
         )
 
     peers = [lax.rem(me + step, n) for step in range(1, n)]
+    up, down = z + 1 < near, z >= 1
+
+    @pl.when(up)
+    def _():
+        chain_copy(x_ref.at[half], z, 0, z + 1).start()
+
+    @pl.when(down)
+    def _():
+        chain_copy(x_ref.at[half], z, 1, z - 1).start()
+
+    for part in range(2):
+        core_copy(x_ref.at[part], z, part, k).start()
     for peer in peers:
         code_copy(peer, me).start()
-    own_code = pltpu.make_async_copy(code_ref, codes_ref.at[me], code_own)
-    own_code.start()
-    x = x_ref[...]
-    factor = 1.0 / math.sqrt(DH)
-    queries = jnp.dot(x, wq_ref[...], preferred_element_type=jnp.float32)
-    queries = (queries.astype(jnp.bfloat16).astype(jnp.float32) * factor).astype(jnp.bfloat16)
-    keys = jnp.dot(x, wk_ref[...], preferred_element_type=jnp.float32).astype(jnp.bfloat16)
-    values = jnp.dot(x, wv_ref[...], preferred_element_type=jnp.float32).astype(jnp.bfloat16)
-    grads = grad_ref[...]
+    loads[3].wait()
+    deep = grads.shape[0] // 2
     for head in range(n):
         cols = slice(head * DH, (head + 1) * DH)
-        outbox[head] = jnp.concatenate(
-            [queries[:, cols], grads[:, cols], keys[:, cols], values[:, cols]], axis=1
-        )
-    for peer in peers:
-        head_copy(peer, me).start()
-    own = pltpu.make_async_copy(outbox.at[me], heads_ref.at[me], own_sem)
+        outbox[head] = jnp.concatenate([grads[:deep, cols], grads[deep:, cols]], axis=1)
+    for peer in peers:
+        grad_copy(peer, me).start()
+    own = pltpu.make_async_copy(outbox.at[me], inbox.at[me], own_sem)
     own.start()
+
+    sides = []
+    for d in range(1, near):
+        sides.append((z - d, z - d >= 0, up, 0, z + 1))
+        sides.append((z + d, z + d < near, down, 1, z - 1))
+
+    def through_row(origin, there):
+        @pl.when(there)
+        def _():
+            block = x_all.at[2 * origin + k, other]
+            row_copy(block, origin, other).wait_recv()
+            core_copy(block, origin, other, k).start()
+
+    for step, (origin, there, onward, side, target) in enumerate(sides):
+        @pl.when(there)
+        def _(origin=origin, onward=onward, side=side, target=target):
+            block = x_all.at[2 * origin + k, half]
+            chain_copy(block, origin, side, z).wait_recv()
+
+            @pl.when(onward)
+            def _():
+                chain_copy(block, origin, side, target).start()
+
+            row_copy(block, origin, half).start()
+            core_copy(block, origin, half, k).start()
+
+        if step >= 2:
+            through_row(*sides[step - 2][:2])
+    for origin, there, _, _, _ in sides[-2:]:
+        through_row(origin, there)
+    for load in loads[:3] + loads[4:]:
+        load.wait()
+    factor = 1.0 / math.sqrt(DH)
+    picked = [
+        jnp.where(k == 0, weights[i, :, :DH], weights[i, :, DH:]) for i in range(3)
+    ]
+    weight = jnp.concatenate([picked[0], picked[0], picked[1], picked[2]], axis=1)
     own.wait()
-    own_code.wait()
+    for origin in range(near):
+        for part in range(2):
+            core_copy(x_all.at[2 * origin + 1 - k, part], origin, part, 1 - k).wait_recv()
     for peer in peers:
         code_copy(peer, peer).wait_recv()
-        head_copy(peer, peer).wait_recv()
+        grad_copy(peer, peer).wait_recv()
+    for panel in range(n):
+        x = x_all[panel].reshape(2 * deep, x_all.shape[3])
+        made = jnp.dot(x, weight, preferred_element_type=jnp.float32).astype(jnp.bfloat16)
+        queries = (made[:, :DH].astype(jnp.float32) * factor).astype(jnp.bfloat16)
+        box = inbox[panel]
+        heads_ref[panel, :deep, : 2 * DH] = jnp.concatenate([queries[:deep], box[:, :DH]], axis=1)
+        heads_ref[panel, deep:, : 2 * DH] = jnp.concatenate([queries[deep:], box[:, DH:]], axis=1)
+        heads_ref[panel, :, 2 * DH :] = made[:, 2 * DH :]
     for peer in peers:
         code_copy(peer, me).wait_send()
-        head_copy(peer, me).wait_send()
+        grad_copy(peer, me).wait_send()
+
+    @pl.when(up)
+    def _():
+        chain_copy(x_ref.at[half], z, 0, z + 1).wait_send()
+
+    @pl.when(down)
+    def _():
+        chain_copy(x_ref.at[half], z, 1, z - 1).wait_send()
+
+    for part in range(2):
+        core_copy(x_ref.at[part], z, part, k).wait_send()
+    for origin, there, onward, side, target in sides:
+        @pl.when(there)
+        def _(origin=origin, onward=onward, side=side, target=target):
+            block = x_all.at[2 * origin + k, half]
+
+            @pl.when(onward)
+            def _():
+                chain_copy(block, origin, side, target).wait_send()
+
+            row_copy(block, origin, half).wait_send()
+            core_copy(block, origin, half, k).wait_send()
+            core_copy(x_all.at[2 * origin + k, other], origin, other, k).wait_send()
 
 
 def spread(node_states, query_weight, key_weight, value_weight, output_grad, codes, n):
-    rows = node_states.shape[0]
+    rows, depth = node_states.shape
     width = 4 * DH
+    near = n // 2
     vmem = pl.BlockSpec(memory_space=pltpu.VMEM)
+    hbm = pl.BlockSpec(memory_space=pltpu.HBM)
+    dma = pltpu.SemaphoreType.DMA
     return pl.pallas_call(
         functools.partial(spread_kernel, n),
         out_shape=(
             jax.ShapeDtypeStruct((n, rows, width), jnp.bfloat16),
             jax.ShapeDtypeStruct((n,) + codes.shape, jnp.int32),
+            jax.ShapeDtypeStruct((n, 2, rows // 2, depth), jnp.bfloat16),
         ),
-        in_specs=[vmem] * 6,
-        out_specs=(pl.BlockSpec(memory_space=pl.ANY), pl.BlockSpec(memory_space=pl.ANY)),
+        in_specs=[hbm] * 5 + [vmem],
+        out_specs=(vmem, vmem, vmem),
         scratch_shapes=[
-            pltpu.VMEM((n, rows, width), jnp.bfloat16),
-            pltpu.SemaphoreType.DMA,
-            pltpu.SemaphoreType.DMA((n,)),
-            pltpu.SemaphoreType.DMA((n,)),
-            pltpu.SemaphoreType.DMA((n,)),
-            pltpu.SemaphoreType.DMA((n,)),
-            pltpu.SemaphoreType.DMA,
+            pltpu.VMEM(output_grad.shape, jnp.bfloat16),
+            pltpu.VMEM((3, depth, 2 * DH), jnp.bfloat16),
+            pltpu.VMEM((n, rows // 2, 2 * DH), jnp.bfloat16),
+            pltpu.VMEM((n, rows // 2, 2 * DH), jnp.bfloat16),
+            dma, dma((6,)), dma((n,)), dma((n,)), dma((n,)), dma((n,)),
+            dma((2, near)), dma((near,)), dma((near, 2)), dma((near, 2)), dma((near,)), dma((near,)),
         ],
         compiler_params=pltpu.CompilerParams(
-            collective_id=0, has_side_effects=True, vmem_limit_bytes=24 << 20
+            collective_id=0, has_side_effects=True, vmem_limit_bytes=16 << 20
         ),
         cost_estimate=pl.CostEstimate(
-            flops=6 * rows * node_states.shape[1] * n * DH, bytes_accessed=40 << 20, transcendentals=0
+            flops=6 * rows * depth * n * DH, bytes_accessed=40 << 20, transcendentals=0
         ),
         name="spread_heads",
-    )(node_states, query_weight, key_weight, value_weight, output_grad, codes)
+    )(
+        node_states.reshape(2, rows // 2, depth), query_weight, key_weight, value_weight,
+        output_grad, codes,
+    )
 
 
 def attend_kernel(
@@ -439,7 +560,7 @@
             pltpu.SMEM((blocks, key_total), jnp.int32),
             pltpu.SMEM((blocks,), jnp.int32),
         ],
-        compiler_params=pltpu.CompilerParams(vmem_limit_bytes=24 << 20),
+        compiler_params=pltpu.CompilerParams(vmem_limit_bytes=16 << 20),
         cost_estimate=pl.CostEstimate(
             flops=tiles * 24 * BLK * BLK * DH, bytes_accessed=80 << 20,
             transcendentals=tiles * BLK * BLK,
@@ -483,19 +604,22 @@
         res_copy(peer, me).start()
     inbox[me] = res_ref[me]
     rows = res_ref.shape[1]
-    chunk = x_ref.shape[1] // n
+    depth = x_ref.shape[3]
+    chunk = depth // n
     turned = res_ref[...].reshape(n * rows, 4 * DH).T
     for peer in range(n):
         term = jnp.dot(
-            turned, x_ref[:, peer * chunk : (peer + 1) * chunk], preferred_element_type=jnp.float32
+            turned,
+            x_ref[:, :, :, peer * chunk : (peer + 1) * chunk].reshape(n * rows, chunk),
+            preferred_element_type=jnp.float32,
         ).astype(jnp.bfloat16)
         terms_out[peer, :DH] = term[:DH]
         terms_out[peer, DH:] = term[2 * DH :]
+    terms_in[me] = terms_out[me]
+    for peer in peers:
+        res_copy(peer, peer).wait_recv()
     for peer in peers:
         term_copy(peer, me).start()
-    terms_in[me] = terms_out[me]
-    for peer in peers:
-        res_copy(peer, peer).wait_recv()
 
     def piece(which):
         return jnp.concatenate(
@@ -542,7 +666,7 @@
 
 def collect_grads(res, x_all, query_weight, key_weight, value_weight, n, n_row):
     rows = res.shape[1]
-    depth = x_all.shape[1]
+    depth = x_all.shape[3]
     cols = depth // n_row
     chunk = depth // n
     head_cols = n * DH
@@ -568,7 +692,7 @@
             dma((n,)), dma((n,)), dma((n,)), dma((n,)), dma((n_row,)), dma((n_row,)),
         ],
         compiler_params=pltpu.CompilerParams(
-            collective_id=1, has_side_effects=True, vmem_limit_bytes=40 << 20
+            collective_id=1, has_side_effects=True, vmem_limit_bytes=20 << 20
         ),
         name="collect_grads",
     )(res, x_all, query_weight, key_weight, value_weight)
@@ -582,8 +706,7 @@
     listed = jnp.pad(pair_list[0].T, ((0, 0), (0, BLK - slots)))
     total = jnp.broadcast_to(pair_count[0], (6, BLK))
     codes = jnp.concatenate([listed, total], axis=0)
-    x_all = lax.all_gather(node_states, "col", axis=0, tiled=True)
-    heads, codes_all = spread(
+    heads, codes_all, x_all = spread(
         node_states, query_weight, key_weight, value_weight, output_grad, codes, n
     )
     res = attend(heads, codes_all, n, blocks)
@@ -594,7 +717,7 @@
     n, n_row = mesh.shape["col"], mesh.shape["row"]
     node_states, query_weight, pair_list = arrays[0], arrays[1], arrays[5]
     blocks = node_states.shape[0] // BLK
-    one_head_each = query_weight.shape[1] == n * DH and n % 2 == 0
+    one_head_each = query_weight.shape[1] == n * DH and n % 2 == 0 and n_row == 2
     tiled = (n * blocks) % GROUP == 0 and pair_list.shape[1] <= BLK
     lanes = node_states.shape[1] % (n * BLK) == 0 and node_states.shape[1] % (n_row * BLK) == 0
     if one_head_each and tiled and lanes:

time: 140 us -> 105 us (0.75)
  the two profiles are of different devices: /device:TPU:25 before, /device:TPU:0 now
where the time goes in v2:
time: 105 us
  Pallas kernels  93.8 us (89%)
  local copies, waits for them, and re-layouts  9.29 us (9%)
  between operations  1.36 us (1%)
    pallas_call x1, Pallas kernels, spread(): pl.pallas_call(functools.partial(spread_kernel, n), out_shape=(jax.ShapeD...  40.7 us
    pallas_call x1, Pallas kernels, collect_grads(): pl.pallas_call(functools.partial(collect_kernel, n, n_row), out_shape=(ja...  36.5 us
    pallas_call x1, Pallas kernels, attend(): pl.pallas_call(functools.partial(attend_kernel, n, blocks), out_shape=jax...  16.5 us
    unnamed x21, local copies, waits for them, and re-layouts  9.29 us

profile of v2, /device:TPU:0, one launch (start us, length us, event | category | flops | bytes accessed | tf_op | source)
XLA Modules:
  0.0 105.1 jit_solution(16475862299814677412)
XLA Ops:
  1.3 0.7 pad_select_fusion.code_ref
  2.0 0.0 copy-start
  2.0 1.2 %copy-done = bf16[1024,512]{1,0:T(8,128)(2,1)S(1)} copy-done((bf16[1024,512]{1,0:T(8,128)(2,1)S(1)}, bf16[1024,512]{1,0:T(8,128)(2,1)}, u32[]{:S(2)}) %copy-start) | copy-done | bytes 1048600
  3.2 0.0 copy-start.2
  3.2 1.2 %copy-done.2 = bf16[1024,512]{1,0:T(8,128)(2,1)S(1)} copy-done((bf16[1024,512]{1,0:T(8,128)(2,1)S(1)}, bf16[1024,512]{1,0:T(8,128)(2,1)}, u32[]{:S(2)}) %copy-start.2) | copy-done | bytes 1048600
  4.4 0.0 copy-start.4
  4.4 1.2 %copy-done.4 = bf16[1024,512]{1,0:T(8,128)(2,1)S(1)} copy-done((bf16[1024,512]{1,0:T(8,128)(2,1)S(1)}, bf16[1024,512]{1,0:T(8,128)(2,1)}, u32[]{:S(2)}) %copy-start.4) | copy-done | bytes 1048600
  5.6 0.0 copy-start.6
  5.6 1.0 copy-done.6
  6.7 0.0 copy-start.7
  6.7 0.9 copy-done.7
  7.6 40.7 %spread_heads.1 = (bf16[8,256,256]{2,1,0:T(8,128)(2,1)S(1)}, s32[8,8,128]{2,1,0:T(8,128)S(1)}, bf16[8,2,128,1024]{3,2,1,0:T(8,128)(2,1)S(1)}) custom-call(bf16[2,128,1024]{2,1,0:T(8,128)(2,1)S(1)} %bitcast.6, bf16[1024,512]{1,0:T(8,128)(2,1)S(1)} %copy-done, bf16[1024,512]{1,0:T(8,128)(2,1)S(1)} %copy-done.2, bf16[1024,512]{1,0:T(8,128)(2,1)S(1)} %copy-done.4, ...), custom_call_target="tpu_custom_call" | custom-call | flops 805306368 | bytes 41943040 | tf_op jit(solution)/shard_map/spread_heads/pallas_call | solution.py:402
  48.4 0.0 copy-start.1
  48.4 0.0 copy-start.3
  48.4 0.0 copy-start.5
  48.4 16.5 %attend_heads.1.res_ref = bf16[8,256,256]{2,1,0:T(8,128)(2,1)S(1)} custom-call(s32[8,8,128]{2,1,0:T(8,128)S(1)} %get-tuple-element.8.codes_ref, bf16[8,256,256]{2,1,0:T(8,128)(2,1)S(1)} %get-tuple-element.9.heads_ref), custom_call_target="tpu_custom_call" | custom-call | flops 6442450944 | bytes 83886080 | tf_op jit(solution)/shard_map/attend_heads/pallas_call | solution.py:548
  65.0 0.0 copy-done.1
  65.0 0.0 copy-done.3
  65.0 0.0 copy-done.5
  65.0 36.5 %collect_grads.1 = (bf16[256,512]{1,0:T(8,128)(2,1)S(1)}, f32[256,512]{1,0:T(8,128)S(1)}, f32[128,512]{1,0:T(8,128)S(1)}, f32[128,512]{1,0:T(8,128)S(1)}, f32[128,512]{1,0:T(8,128)S(1)}) custom-call(bf16[8,256,256]{2,1,0:T(8,128)(2,1)S(1)} %attend_heads.1.res_ref, bf16[8,2,128,1024]{3,2,1,0:T(8,128)(2,1)S(1)} %get-tuple-element.10.x_ref, ...), custom_call_target="tpu_custom_call" | custom-call | tf_op jit(solution)/shard_map/collect_grads/pallas_call | solution.py:675
  101.5 0.7 copy.18
  102.2 0.8 copy.19
  103.0 0.7 copy.20
  103.7 0.7 copy.21
  104.4 0.7 copy.22
Async XLA Ops:
  2.0 1.2 %copy-start = (bf16[1024,512]{1,0:T(8,128)(2,1)S(1)}, bf16[1024,512]{1,0:T(8,128)(2,1)}, u32[]{:S(2)}) copy-start(bf16[1024,512]{1,0:T(8,128)(2,1)} %wq_ref.3) | copy-start | bytes 3145732
  3.2 1.2 %copy-start.2 = (bf16[1024,512]{1,0:T(8,128)(2,1)S(1)}, bf16[1024,512]{1,0:T(8,128)(2,1)}, u32[]{:S(2)}) copy-start(bf16[1024,512]{1,0:T(8,128)(2,1)} %wk_ref.3) | copy-start | bytes 3145732
  4.4 1.2 %copy-start.4 = (bf16[1024,512]{1,0:T(8,128)(2,1)S(1)}, bf16[1024,512]{1,0:T(8,128)(2,1)}, u32[]{:S(2)}) copy-start(bf16[1024,512]{1,0:T(8,128)(2,1)} %wv_ref.3) | copy-start | bytes 3145732
  5.6 1.0 copy-start.6
  6.7 0.9 copy-start.7
  48.4 16.6 %copy-start.1 = (bf16[1024,512]{1,0:T(8,128)(2,1)S(1)}, bf16[1024,512]{1,0:T(8,128)(2,1)}, u32[]{:S(2)}) copy-start(bf16[1024,512]{1,0:T(8,128)(2,1)} %wq_ref.3) | copy-start | bytes 3145732
  48.4 16.6 %copy-start.3 = (bf16[1024,512]{1,0:T(8,128)(2,1)S(1)}, bf16[1024,512]{1,0:T(8,128)(2,1)}, u32[]{:S(2)}) copy-start(bf16[1024,512]{1,0:T(8,128)(2,1)} %wk_ref.3) | copy-start | bytes 3145732
  48.4 16.6 %copy-start.5 = (bf16[1024,512]{1,0:T(8,128)(2,1)S(1)}, bf16[1024,512]{1,0:T(8,128)(2,1)}, u32[]{:S(2)}) copy-start(bf16[1024,512]{1,0:T(8,128)(2,1)} %wv_ref.3) | copy-start | bytes 3145732

commit v3 on v2

--- a/solution.py
+++ b/solution.py
@@ -213,6 +213,7 @@
 
 MESH = pl.DeviceIdType.MESH
 GROUP = 4
+CUTS = 2
 
 
 def meet(axes):
@@ -228,8 +229,8 @@
 
 
 def spread_kernel(
-    n, x_ref, wq_ref, wk_ref, wv_ref, grad_ref, code_ref, heads_ref, codes_ref, x_all,
-    grads, weights, outbox, inbox, own_sem, load_sem, grad_send, grad_recv, code_send, code_recv,
+    n, x_ref, wq_ref, wk_ref, wv_ref, grad_ref, code_ref, heads_ref, codes_ref, x_out,
+    x_all, keep_sem, grads, weights, weight, outbox, inbox, load_sem, grad_send, grad_recv, code_send, code_recv,
     chain_send, chain_recv, core_send, core_recv, row_send, row_recv,
 ):
     me = lax.axis_index("col")
@@ -267,10 +268,10 @@
             recv_sem=grad_recv.at[slot], device_id={"col": peer}, device_id_type=MESH,
         )
 
-    def chain_copy(src, origin, side, target):
+    def chain_copy(src, origin, cut, side, target):
         return pltpu.make_async_remote_copy(
-            src_ref=src, dst_ref=x_all.at[2 * origin + k, half],
-            send_sem=chain_send.at[side, origin], recv_sem=chain_recv.at[origin],
+            src_ref=src, dst_ref=x_all.at[2 * origin + k, half * CUTS + cut],
+            send_sem=chain_send.at[side, origin, cut], recv_sem=chain_recv.at[origin, cut],
             device_id={"col": 2 * target + k}, device_id_type=MESH,
         )
 
@@ -281,25 +282,28 @@
             device_id={"col": twin}, device_id_type=MESH,
         )
 
-    def row_copy(src, origin, part):
+    def row_copy(src, origin, cut, part):
         return pltpu.make_async_remote_copy(
-            src_ref=src, dst_ref=x_all.at[2 * origin + k, part],
-            send_sem=row_send.at[origin], recv_sem=row_recv.at[origin],
+            src_ref=src, dst_ref=x_all.at[2 * origin + k, part * CUTS + cut],
+            send_sem=row_send.at[origin, cut], recv_sem=row_recv.at[origin, cut],
             device_id={"row": other}, device_id_type=MESH,
         )
 
     peers = [lax.rem(me + step, n) for step in range(1, n)]
     up, down = z + 1 < near, z >= 1
 
-    @pl.when(up)
-    def _():
-        chain_copy(x_ref.at[half], z, 0, z + 1).start()
-
-    @pl.when(down)
-    def _():
-        chain_copy(x_ref.at[half], z, 1, z - 1).start()
-
-    for part in range(2):
+    for cut in range(CUTS):
+        piece = x_ref.at[half * CUTS + cut]
+
+        @pl.when(up)
+        def _(piece=piece, cut=cut):
+            chain_copy(piece, z, cut, 0, z + 1).start()
+
+        @pl.when(down)
+        def _(piece=piece, cut=cut):
+            chain_copy(piece, z, cut, 1, z - 1).start()
+
+    for part in range(2 * CUTS):
         core_copy(x_ref.at[part], z, part, k).start()
     for peer in peers:
         code_copy(peer, me).start()
@@ -310,86 +314,112 @@
         outbox[head] = jnp.concatenate([grads[:deep, cols], grads[deep:, cols]], axis=1)
     for peer in peers:
         grad_copy(peer, me).start()
-    own = pltpu.make_async_copy(outbox.at[me], inbox.at[me], own_sem)
-    own.start()
-
-    sides = []
-    for d in range(1, near):
-        sides.append((z - d, z - d >= 0, up, 0, z + 1))
-        sides.append((z + d, z + d < near, down, 1, z - 1))
-
-    def through_row(origin, there):
-        @pl.when(there)
-        def _():
-            block = x_all.at[2 * origin + k, other]
-            row_copy(block, origin, other).wait_recv()
-            core_copy(block, origin, other, k).start()
-
-    for step, (origin, there, onward, side, target) in enumerate(sides):
-        @pl.when(there)
-        def _(origin=origin, onward=onward, side=side, target=target):
-            block = x_all.at[2 * origin + k, half]
-            chain_copy(block, origin, side, z).wait_recv()
-
-            @pl.when(onward)
-            def _():
-                chain_copy(block, origin, side, target).start()
-
-            row_copy(block, origin, half).start()
-            core_copy(block, origin, half, k).start()
-
-        if step >= 2:
-            through_row(*sides[step - 2][:2])
-    for origin, there, _, _, _ in sides[-2:]:
-        through_row(origin, there)
+    inbox[me] = outbox[me]
     for load in loads[:3] + loads[4:]:
         load.wait()
     factor = 1.0 / math.sqrt(DH)
     picked = [
         jnp.where(k == 0, weights[i, :, :DH], weights[i, :, DH:]) for i in range(3)
     ]
-    weight = jnp.concatenate([picked[0], picked[0], picked[1], picked[2]], axis=1)
-    own.wait()
-    for origin in range(near):
-        for part in range(2):
+    for place, i in enumerate((0, 0, 1, 2)):
+        weight[:, place * DH : (place + 1) * DH] = picked[i]
+
+    def keep(origin):
+        pair = pl.ds(2 * origin, 2)
+        return pltpu.make_async_copy(x_all.at[pair], x_out.at[pair], keep_sem.at[origin])
+
+    def project(origin):
+        for part in range(2 * CUTS):
             core_copy(x_all.at[2 * origin + 1 - k, part], origin, part, 1 - k).wait_recv()
+        keep(origin).start()
+        for core in range(2):
+            panel = 2 * origin + core
+            x = x_all[panel].reshape(2 * deep, x_all.shape[3])
+            made = jnp.dot(x, weight[...], preferred_element_type=jnp.float32)
+            made = made.astype(jnp.bfloat16)
+            queries = (made[:, :DH].astype(jnp.float32) * factor).astype(jnp.bfloat16)
+            heads_ref[panel, :, :DH] = queries
+            heads_ref[panel, :, 2 * DH :] = made[:, 2 * DH :]
+
+    def through_row(origin, cut, there):
+        @pl.when(there)
+        def _():
+            block = x_all.at[2 * origin + k, other * CUTS + cut]
+            row_copy(block, origin, cut, other).wait_recv()
+            core_copy(block, origin, other * CUTS + cut, k).start()
+
+    def onto(origin, cut, there, onward, side, target):
+        @pl.when(there)
+        def _():
+            block = x_all.at[2 * origin + k, half * CUTS + cut]
+            chain_copy(block, origin, cut, side, z).wait_recv()
+
+            @pl.when(onward)
+            def _():
+                chain_copy(block, origin, cut, side, target).start()
+
+            row_copy(block, origin, cut, half).start()
+            core_copy(block, origin, half * CUTS + cut, k).start()
+
+    steps = []
+    for d in range(1, near):
+        for cut in range(CUTS):
+            steps.append((z - d, cut, z - d >= 0, up, 0, z + 1))
+            steps.append((z + d, cut, z + d < near, down, 1, z - 1))
+    each = 2 * CUTS
+    for step, (origin, cut, there, onward, side, target) in enumerate(steps):
+        onto(origin, cut, there, onward, side, target)
+        if step >= 2:
+            through_row(*steps[step - 2][:3])
+        if step == each - 1:
+            project(z)
+        if step == each + 1:
+            for peer in peers:
+                grad_copy(peer, peer).wait_recv()
+            for panel in range(n):
+                heads_ref[panel, :deep, DH : 2 * DH] = inbox[panel, :, :DH]
+                heads_ref[panel, deep:, DH : 2 * DH] = inbox[panel, :, DH:]
+        if step >= 2 * each - 1 and (step + 1) % each == 0:
+            for origin, _, there, _, _, _ in steps[step - 2 * each + 1 : step - 2 * each + 3]:
+                pl.when(there)(functools.partial(project, origin))
+    for origin, cut, there, _, _, _ in steps[-2:]:
+        through_row(origin, cut, there)
+    for origin, _, there, _, _, _ in steps[-2:]:
+        pl.when(there)(functools.partial(project, origin))
     for peer in peers:
         code_copy(peer, peer).wait_recv()
-        grad_copy(peer, peer).wait_recv()
-    for panel in range(n):
-        x = x_all[panel].reshape(2 * deep, x_all.shape[3])
-        made = jnp.dot(x, weight, preferred_element_type=jnp.float32).astype(jnp.bfloat16)
-        queries = (made[:, :DH].astype(jnp.float32) * factor).astype(jnp.bfloat16)
-        box = inbox[panel]
-        heads_ref[panel, :deep, : 2 * DH] = jnp.concatenate([queries[:deep], box[:, :DH]], axis=1)
-        heads_ref[panel, deep:, : 2 * DH] = jnp.concatenate([queries[deep:], box[:, DH:]], axis=1)
-        heads_ref[panel, :, 2 * DH :] = made[:, 2 * DH :]
+    for origin in range(near):
+        keep(origin).wait()
     for peer in peers:
         code_copy(peer, me).wait_send()
         grad_copy(peer, me).wait_send()
-
-    @pl.when(up)
-    def _():
-        chain_copy(x_ref.at[half], z, 0, z + 1).wait_send()
-
-    @pl.when(down)
-    def _():
-        chain_copy(x_ref.at[half], z, 1, z - 1).wait_send()
-
-    for part in range(2):
+    for cut in range(CUTS):
+        piece = x_ref.at[half * CUTS + cut]
+
+        @pl.when(up)
+        def _(piece=piece, cut=cut):
+            chain_copy(piece, z, cut, 0, z + 1).wait_send()
+
+        @pl.when(down)
+        def _(piece=piece, cut=cut):
+            chain_copy(piece, z, cut, 1, z - 1).wait_send()
+
+    for part in range(2 * CUTS):
         core_copy(x_ref.at[part], z, part, k).wait_send()
-    for origin, there, onward, side, target in sides:
+    for origin, cut, there, onward, side, target in steps:
         @pl.when(there)
-        def _(origin=origin, onward=onward, side=side, target=target):
-            block = x_all.at[2 * origin + k, half]
+        def _(origin=origin, cut=cut, onward=onward, side=side, target=target):
+            block = x_all.at[2 * origin + k, half * CUTS + cut]
 
             @pl.when(onward)
             def _():
-                chain_copy(block, origin, side, target).wait_send()
-
-            row_copy(block, origin, half).wait_send()
-            core_copy(block, origin, half, k).wait_send()
-            core_copy(x_all.at[2 * origin + k, other], origin, other, k).wait_send()
+                chain_copy(block, origin, cut, side, target).wait_send()
+
+            row_copy(block, origin, cut, half).wait_send()
+            core_copy(block, origin, half * CUTS + cut, k).wait_send()
+            core_copy(
+                x_all.at[2 * origin + k, other * CUTS + cut], origin, other * CUTS + cut, k
+            ).wait_send()
 
 
 def spread(node_states, query_weight, key_weight, value_weight, output_grad, codes, n):
@@ -404,27 +434,31 @@
         out_shape=(
             jax.ShapeDtypeStruct((n, rows, width), jnp.bfloat16),
             jax.ShapeDtypeStruct((n,) + codes.shape, jnp.int32),
-            jax.ShapeDtypeStruct((n, 2, rows // 2, depth), jnp.bfloat16),
+            jax.ShapeDtypeStruct((n, 2 * CUTS, rows // (2 * CUTS), depth), jnp.bfloat16),
         ),
         in_specs=[hbm] * 5 + [vmem],
-        out_specs=(vmem, vmem, vmem),
+        out_specs=(vmem, vmem, hbm),
         scratch_shapes=[
+            pltpu.VMEM((n, 2 * CUTS, rows // (2 * CUTS), depth), jnp.bfloat16),
+            dma((near,)),
             pltpu.VMEM(output_grad.shape, jnp.bfloat16),
             pltpu.VMEM((3, depth, 2 * DH), jnp.bfloat16),
+            pltpu.VMEM((depth, 4 * DH), jnp.bfloat16),
             pltpu.VMEM((n, rows // 2, 2 * DH), jnp.bfloat16),
             pltpu.VMEM((n, rows // 2, 2 * DH), jnp.bfloat16),
-            dma, dma((6,)), dma((n,)), dma((n,)), dma((n,)), dma((n,)),
-            dma((2, near)), dma((near,)), dma((near, 2)), dma((near, 2)), dma((near,)), dma((near,)),
+            dma((6,)), dma((n,)), dma((n,)), dma((n,)), dma((n,)),
+            dma((2, near, CUTS)), dma((near, CUTS)), dma((near, 2 * CUTS)),
+            dma((near, 2 * CUTS)), dma((near, CUTS)), dma((near, CUTS)),
         ],
         compiler_params=pltpu.CompilerParams(
-            collective_id=0, has_side_effects=True, vmem_limit_bytes=16 << 20
+            collective_id=0, has_side_effects=True, vmem_limit_bytes=54 << 20
         ),
         cost_estimate=pl.CostEstimate(
             flops=6 * rows * depth * n * DH, bytes_accessed=40 << 20, transcendentals=0
         ),
         name="spread_heads",
     )(
-        node_states.reshape(2, rows // 2, depth), query_weight, key_weight, value_weight,
+        node_states.reshape(2 * CUTS, rows // (2 * CUTS), depth), query_weight, key_weight, value_weight,
         output_grad, codes,
     )
 
@@ -571,8 +605,8 @@
 
 def collect_kernel(
     n, n_row, res_ref, x_ref, wq_ref, wk_ref, wv_ref,
-    att_ref, node_ref, qg_ref, kg_ref, vg_ref,
-    inbox, terms_out, terms_in, part_out, part_in,
+    att_ref, terms_in, part_in,
+    inbox, terms_out, part_out,
     send_sem, recv_sem, term_send, term_recv, row_send, row_recv,
 ):
     me = lax.axis_index("col")
@@ -642,26 +676,42 @@
     att_ref[...] = piece(1)
     for peer in peers:
         term_copy(peer, peer).wait_recv()
-    for which, ref in enumerate((qg_ref, kg_ref, vg_ref)):
-        for h in range(0, n, 2):
-            pair = jnp.concatenate(
-                [
-                    terms_in[h, which * DH : (which + 1) * DH],
-                    terms_in[h + 1, which * DH : (which + 1) * DH],
-                ],
-                axis=0,
-            )
-            ref[:, h * DH : (h + 2) * DH] = pair.astype(jnp.float32).T
-    total = part_out[my_row].astype(jnp.float32)
+    part_in[my_row] = part_out[my_row]
     for peer in row_peers:
         row_copy(peer, peer).wait_recv()
-        total = total + part_in[peer].astype(jnp.float32)
-    node_ref[...] = total
     for peer in peers:
         res_copy(peer, me).wait_send()
         term_copy(peer, me).wait_send()
     for peer in row_peers:
         row_copy(peer, my_row).wait_send()
+
+
+def finish_kernel(
+    n, n_row, att_in, terms, parts, att_ref, node_ref, qg_ref, kg_ref, vg_ref,
+    node_buf, grad_buf, sem,
+):
+    copies = [pltpu.make_async_copy(att_in, att_ref, sem.at[0])]
+    copies[0].start()
+    total = parts[0].astype(jnp.float32)
+    for r in range(1, n_row):
+        total = total + parts[r].astype(jnp.float32)
+    node_buf[...] = total
+    copies.append(pltpu.make_async_copy(node_buf, node_ref, sem.at[1]))
+    copies[1].start()
+    for which, ref in enumerate((qg_ref, kg_ref, vg_ref)):
+        for h in range(0, n, 2):
+            pair = jnp.concatenate(
+                [
+                    terms[h, which * DH : (which + 1) * DH],
+                    terms[h + 1, which * DH : (which + 1) * DH],
+                ],
+                axis=0,
+            )
+            grad_buf[which, :, h * DH : (h + 2) * DH] = pair.astype(jnp.float32).T
+        copies.append(pltpu.make_async_copy(grad_buf.at[which], ref, sem.at[2 + which]))
+        copies[-1].start()
+    for copy in copies:
+        copy.wait()
 
 
 def collect_grads(res, x_all, query_weight, key_weight, value_weight, n, n_row):
@@ -671,23 +721,20 @@
     chunk = depth // n
     head_cols = n * DH
     vmem = pl.BlockSpec(memory_space=pltpu.VMEM)
+    hbm = pl.BlockSpec(memory_space=pltpu.HBM)
     dma = pltpu.SemaphoreType.DMA
-    return pl.pallas_call(
+    att, terms, parts = pl.pallas_call(
         functools.partial(collect_kernel, n, n_row),
         out_shape=(
             jax.ShapeDtypeStruct((rows, head_cols), jnp.bfloat16),
-            jax.ShapeDtypeStruct((rows, cols), jnp.float32),
-            jax.ShapeDtypeStruct((chunk, head_cols), jnp.float32),
-            jax.ShapeDtypeStruct((chunk, head_cols), jnp.float32),
-            jax.ShapeDtypeStruct((chunk, head_cols), jnp.float32),
+            jax.ShapeDtypeStruct((n, 3 * DH, chunk), jnp.bfloat16),
+            jax.ShapeDtypeStruct((n_row, rows, cols), jnp.bfloat16),
         ),
         in_specs=[vmem] * 5,
-        out_specs=(vmem,) * 5,
+        out_specs=(vmem,) * 3,
         scratch_shapes=[
             pltpu.VMEM(res.shape, jnp.bfloat16),
             pltpu.VMEM((n, 3 * DH, chunk), jnp.bfloat16),
-            pltpu.VMEM((n, 3 * DH, chunk), jnp.bfloat16),
-            pltpu.VMEM((n_row, rows, cols), jnp.bfloat16),
             pltpu.VMEM((n_row, rows, cols), jnp.bfloat16),
             dma((n,)), dma((n,)), dma((n,)), dma((n,)), dma((n_row,)), dma((n_row,)),
         ],
@@ -696,6 +743,25 @@
         ),
         name="collect_grads",
     )(res, x_all, query_weight, key_weight, value_weight)
+    return pl.pallas_call(
+        functools.partial(finish_kernel, n, n_row),
+        out_shape=(
+            jax.ShapeDtypeStruct((rows, head_cols), jnp.bfloat16),
+            jax.ShapeDtypeStruct((rows, cols), jnp.float32),
+            jax.ShapeDtypeStruct((chunk, head_cols), jnp.float32),
+            jax.ShapeDtypeStruct((chunk, head_cols), jnp.float32),
+            jax.ShapeDtypeStruct((chunk, head_cols), jnp.float32),
+        ),
+        in_specs=[vmem] * 3,
+        out_specs=(hbm,) * 5,
+        scratch_shapes=[
+            pltpu.VMEM((rows, cols), jnp.float32),
+            pltpu.VMEM((3, chunk, head_cols), jnp.float32),
+            dma((5,)),
+        ],
+        compiler_params=pltpu.CompilerParams(vmem_limit_bytes=16 << 20),
+        name="finish",
+    )(att, terms, parts)
 
 
 def per_device_heads(

time: 105 us -> 93.7 us (0.89)
  local copies, waits for them, and re-layouts: 9.29 us -> 1.99 us
  Pallas kernels: 93.8 us -> 88 us
    unnamed x21 -> x12, local copies, waits for them, and re-layouts: 9.29 us -> 1.99 us
    pallas_call x1, Pallas kernels: 40.7 us -> 37.1 us  [spread(): pl.pallas_call(functools.partial(spread_kernel, n), out_shape=(jax.ShapeD...]
    pallas_call x1, Pallas kernels: 16.5 us -> 13.4 us  [attend(): pl.pallas_call(functools.partial(attend_kernel, n, blocks), out_shape=jax...]
    pallas_call x0 -> x1, Pallas kernels: none -> 1.24 us  [collect_grads(): pl.pallas_call(functools.partial(finish_kernel, n, n_row), out_shape=(jax...]
where the time goes in v3:
time: 93.7 us; the launch traced here: 92.8 us
  Pallas kernels  88 us (94%)
  local copies, waits for them, and re-layouts  1.99 us (2%)
  between operations  1.51 us (2%)
  other arithmetic  1.28 us (1%)
    pallas_call x1, Pallas kernels, spread(): pl.pallas_call(functools.partial(spread_kernel, n), out_shape=(jax.ShapeD...  37.1 us
    pallas_call x1, Pallas kernels, collect_grads(): pl.pallas_call(functools.partial(collect_kernel, n, n_row), out_shape=(ja...  36.2 us
    pallas_call x1, Pallas kernels, attend(): pl.pallas_call(functools.partial(attend_kernel, n, blocks), out_shape=jax...  13.4 us
    unnamed x12, local copies, waits for them, and re-layouts  1.99 us

profile of v3, /device:TPU:0, one launch (start us, length us, event | category | flops | bytes accessed | tf_op | source)
XLA Modules:
  0.0 92.8 jit_solution(18412414269467139175)
XLA Ops:
  1.3 1.3 %pad_select_fusion.code_ref = s32[8,128]{1,0:T(8,128)} fusion(s32[2,32]{1,0:T(2,128)} %bitcast.7, s32[]{:T(128)} %bitcast.5), kind=kLoop, calls=%fused_computation.1 | loop fusion | flops 2048 | bytes 4356 | tf_op jit(solution)/shard_map/concatenate | solution.py:774
  2.6 37.1 %spread_heads.1 = (bf16[8,256,256]{2,1,0:T(8,128)(2,1)}, s32[8,8,128]{2,1,0:T(8,128)}, bf16[8,4,64,1024]{3,2,1,0:T(8,128)(2,1)}) custom-call(bf16[4,64,1024]{2,1,0:T(8,128)(2,1)} %bitcast.6, bf16[1024,512]{1,0:T(8,128)(2,1)} %wq_ref.3, bf16[1024,512]{1,0:T(8,128)(2,1)} %wk_ref.3, bf16[1024,512]{1,0:T(8,128)(2,1)} %wv_ref.3, bf16[256,512]{1,0:T(8,128)(2,1)} %grad_ref.1, ...), custom_call_target="tpu_custom_call" | custom-call | flops 805306368 | bytes 41943040 | tf_op jit(solution)/shard_map/spread_heads/pallas_call | solution.py:432
  39.7 0.0 copy-start.4
  39.7 1.2 %copy-done.4 = bf16[8,256,256]{2,1,0:T(8,128)(2,1)S(1)} copy-done((bf16[8,256,256]{2,1,0:T(8,128)(2,1)S(1)}, bf16[8,256,256]{2,1,0:T(8,128)(2,1)}, u32[]{:S(2)}) %copy-start.4) | copy-done | bytes 1048600
  40.9 0.0 copy-start.5
  40.9 0.8 copy-done.5
  41.7 0.0 copy-start
  41.7 0.0 copy-start.1
  41.7 0.0 copy-start.2
  41.7 0.0 copy-start.3
  41.7 13.4 %attend_heads.1.res_ref = bf16[8,256,256]{2,1,0:T(8,128)(2,1)S(1)} custom-call(s32[8,8,128]{2,1,0:T(8,128)S(1)} %copy-done.5, bf16[8,256,256]{2,1,0:T(8,128)(2,1)S(1)} %copy-done.4), custom_call_target="tpu_custom_call" | custom-call | flops 6442450944 | bytes 83886080 | tf_op jit(solution)/shard_map/attend_heads/pallas_call | solution.py:582
  55.1 0.0 copy-done
  55.2 0.0 copy-done.1
  55.2 0.0 copy-done.2
  55.2 0.0 copy-done.3
  55.2 36.2 %collect_grads.1 = (bf16[256,512]{1,0:T(8,128)(2,1)S(1)}, bf16[8,192,128]{2,1,0:T(8,128)(2,1)S(1)}, bf16[2,256,512]{2,1,0:T(8,128)(2,1)S(1)}) custom-call(bf16[8,256,256]{2,1,0:T(8,128)(2,1)S(1)} %attend_heads.1.res_ref, bf16[8,4,64,1024]{3,2,1,0:T(8,128)(2,1)S(1)} %copy-done, bf16[1024,512]{1,0:T(8,128)(2,1)S(1)} %copy-done.1, ...), custom_call_target="tpu_custom_call" | custom-call | tf_op jit(solution)/shard_map/collect_grads/pallas_call | solution.py:726
  91.4 1.2 %finish.1 = (bf16[256,512]{1,0:T(8,128)(2,1)}, f32[256,512]{1,0:T(8,128)}, f32[128,512]{1,0:T(8,128)}, f32[128,512]{1,0:T(8,128)}, f32[128,512]{1,0:T(8,128)}) custom-call(bf16[256,512]{1,0:T(8,128)(2,1)S(1)} %get-tuple-element.14.att_in, bf16[8,192,128]{2,1,0:T(8,128)(2,1)S(1)} %get-tuple-element.15.terms, bf16[2,256,512]{2,1,0:T(8,128)(2,1)S(1)} %get-tuple-element.16.parts), custom_call_target="tpu_custom_call" | custom-call | tf_op jit(solution)/shard_map/finish/pallas_call | solution.py:746
Async XLA Ops:
  39.7 1.2 %copy-start.4 = (bf16[8,256,256]{2,1,0:T(8,128)(2,1)S(1)}, bf16[8,256,256]{2,1,0:T(8,128)(2,1)}, u32[]{:S(2)}) copy-start(bf16[8,256,256]{2,1,0:T(8,128)(2,1)} %get-tuple-element.12.heads_ref) | copy-start | bytes 3145732
  40.9 0.8 copy-start.5
  41.7 13.5 %copy-start = (bf16[8,4,64,1024]{3,2,1,0:T(8,128)(2,1)S(1)}, bf16[8,4,64,1024]{3,2,1,0:T(8,128)(2,1)}, u32[]{:S(2)}) copy-start(bf16[8,4,64,1024]{3,2,1,0:T(8,128)(2,1)} %get-tuple-element.13.x_ref) | copy-start | bytes 12582916
  41.7 13.5 %copy-start.1 = (bf16[1024,512]{1,0:T(8,128)(2,1)S(1)}, bf16[1024,512]{1,0:T(8,128)(2,1)}, u32[]{:S(2)}) copy-start(bf16[1024,512]{1,0:T(8,128)(2,1)} %wq_ref.3) | copy-start | bytes 3145732
  41.7 13.5 %copy-start.2 = (bf16[1024,512]{1,0:T(8,128)(2,1)S(1)}, bf16[1024,512]{1,0:T(8,128)(2,1)}, u32[]{:S(2)}) copy-start(bf16[1024,512]{1,0:T(8,128)(2,1)} %wk_ref.3) | copy-start | bytes 3145732
  41.7 13.5 %copy-start.3 = (bf16[1024,512]{1,0:T(8,128)(2,1)S(1)}, bf16[1024,512]{1,0:T(8,128)(2,1)}, u32[]{:S(2)}) copy-start(bf16[1024,512]{1,0:T(8,128)(2,1)} %wv_ref.3) | copy-start | bytes 3145732

commit v4 on v3

--- a/solution.py
+++ b/solution.py
@@ -212,7 +212,7 @@
 
 
 MESH = pl.DeviceIdType.MESH
-GROUP = 4
+GROUP = 2
 CUTS = 2
 
 
@@ -312,8 +312,6 @@
     for head in range(n):
         cols = slice(head * DH, (head + 1) * DH)
         outbox[head] = jnp.concatenate([grads[:deep, cols], grads[deep:, cols]], axis=1)
-    for peer in peers:
-        grad_copy(peer, me).start()
     inbox[me] = outbox[me]
     for load in loads[:3] + loads[4:]:
         load.wait()
@@ -369,21 +367,23 @@
     each = 2 * CUTS
     for step, (origin, cut, there, onward, side, target) in enumerate(steps):
         onto(origin, cut, there, onward, side, target)
-        if step >= 2:
-            through_row(*steps[step - 2][:3])
+        if step == min(2 * each, len(steps)) - 1:
+            for peer in peers:
+                grad_copy(peer, me).start()
+        if step >= each:
+            through_row(*steps[step - each][:3])
         if step == each - 1:
             project(z)
-        if step == each + 1:
-            for peer in peers:
-                grad_copy(peer, peer).wait_recv()
-            for panel in range(n):
-                heads_ref[panel, :deep, DH : 2 * DH] = inbox[panel, :, :DH]
-                heads_ref[panel, deep:, DH : 2 * DH] = inbox[panel, :, DH:]
         if step >= 2 * each - 1 and (step + 1) % each == 0:
             for origin, _, there, _, _, _ in steps[step - 2 * each + 1 : step - 2 * each + 3]:
                 pl.when(there)(functools.partial(project, origin))
-    for origin, cut, there, _, _, _ in steps[-2:]:
+    for origin, cut, there, _, _, _ in steps[-each:]:
         through_row(origin, cut, there)
+    for peer in peers:
+        grad_copy(peer, peer).wait_recv()
+    for panel in range(n):
+        heads_ref[panel, :deep, DH : 2 * DH] = inbox[panel, :, :DH]
+        heads_ref[panel, deep:, DH : 2 * DH] = inbox[panel, :, DH:]
     for origin, _, there, _, _, _ in steps[-2:]:
         pl.when(there)(functools.partial(project, origin))
     for peer in peers:
@@ -464,7 +464,7 @@
 
 
 def attend_kernel(
-    n, blocks, codes_ref, heads_ref, out_ref, pairs_acc, scores_buf, grads_buf, found, counts
+    n, blocks, codes_ref, heads_ref, out_ref, pairs_acc, scores_buf, grads_buf, kept, found, counts
 ):
     lanes = lax.broadcasted_iota(jnp.int32, (BLK, 2 * DH), 1)
     first = lanes < DH
@@ -531,6 +531,7 @@
             out = jnp.zeros((BLK, 2 * DH), jnp.float32)
             for g in range(groups):
                 weights = (scores_buf[q, g] * totals[q]).astype(jnp.bfloat16)
+                kept[q, g] = weights
                 out = out + jnp.dot(weights, table(q, g), preferred_element_type=jnp.float32)
             outs.append(out)
             grad = stacks[q][BLK:].astype(jnp.float32)
@@ -539,7 +540,7 @@
             rows_grad = jnp.zeros((BLK, 2 * DH), jnp.float32)
             turned = stacks[q].T
             for g in range(groups):
-                weights = (scores_buf[q, g] * totals[q]).astype(jnp.bfloat16)
+                weights = kept[q, g]
                 score_grad = (
                     weights.astype(jnp.float32) * (grads_buf[q, g] - deltas[q])
                 ).astype(jnp.bfloat16)
@@ -591,6 +592,7 @@
             pltpu.VMEM((key_total, 2 * DH, BLK), jnp.float32),
             pltpu.VMEM((blocks, groups, BLK, GROUP * BLK), jnp.float32),
             pltpu.VMEM((blocks, groups, BLK, GROUP * BLK), jnp.float32),
+            pltpu.VMEM((blocks, groups, BLK, GROUP * BLK), jnp.bfloat16),
             pltpu.SMEM((blocks, key_total), jnp.int32),
             pltpu.SMEM((blocks,), jnp.int32),
         ],

time: 93.7 us -> 91.7 us (0.979)
  Pallas kernels: 88 us -> 86.1 us
    pallas_call x1, Pallas kernels: 37.1 us -> 35.9 us  [spread(): pl.pallas_call(functools.partial(spread_kernel, n), out_shape=(jax.ShapeD...]
    pallas_call x1, Pallas kernels: 36.2 us -> 35.1 us  [collect_grads(): pl.pallas_call(functools.partial(collect_kernel, n, n_row), out_shape=(ja...]
where the time goes in v4:
time: 91.7 us; the launch traced here: 90.9 us
  Pallas kernels  86.1 us (94%)
  local copies, waits for them, and re-layouts  1.99 us (2%)
  between operations  1.53 us (2%)
  other arithmetic  1.28 us (1%)
    pallas_call x1, Pallas kernels, spread(): pl.pallas_call(functools.partial(spread_kernel, n), out_shape=(jax.ShapeD...  35.9 us
    pallas_call x1, Pallas kernels, collect_grads(): pl.pallas_call(functools.partial(collect_kernel, n, n_row), out_shape=(ja...  35.1 us
    pallas_call x1, Pallas kernels, attend(): pl.pallas_call(functools.partial(attend_kernel, n, blocks), out_shape=jax...  13.8 us
    unnamed x12, local copies, waits for them, and re-layouts  1.99 us

profile of v4, /device:TPU:0, one launch (start us, length us, event | category | flops | bytes accessed | tf_op | source)
XLA Modules:
  0.0 90.9 jit_solution(11618049182808443640)
XLA Ops:
  1.3 1.3 %pad_select_fusion.code_ref = s32[8,128]{1,0:T(8,128)} fusion(s32[2,32]{1,0:T(2,128)} %bitcast.7, s32[]{:T(128)} %bitcast.5), kind=kLoop, calls=%fused_computation.1 | loop fusion | flops 2048 | bytes 4356 | tf_op jit(solution)/shard_map/concatenate | solution.py:776
  2.6 35.9 %spread_heads.1 = (bf16[8,256,256]{2,1,0:T(8,128)(2,1)}, s32[8,8,128]{2,1,0:T(8,128)}, bf16[8,4,64,1024]{3,2,1,0:T(8,128)(2,1)}) custom-call(bf16[4,64,1024]{2,1,0:T(8,128)(2,1)} %bitcast.6, bf16[1024,512]{1,0:T(8,128)(2,1)} %wq_ref.3, bf16[1024,512]{1,0:T(8,128)(2,1)} %wk_ref.3, bf16[1024,512]{1,0:T(8,128)(2,1)} %wv_ref.3, bf16[256,512]{1,0:T(8,128)(2,1)} %grad_ref.1, ...), custom_call_target="tpu_custom_call" | custom-call | flops 805306368 | bytes 41943040 | tf_op jit(solution)/shard_map/spread_heads/pallas_call | solution.py:432
  38.5 0.0 copy-start.4
  38.5 1.2 %copy-done.4 = bf16[8,256,256]{2,1,0:T(8,128)(2,1)S(1)} copy-done((bf16[8,256,256]{2,1,0:T(8,128)(2,1)S(1)}, bf16[8,256,256]{2,1,0:T(8,128)(2,1)}, u32[]{:S(2)}) %copy-start.4) | copy-done | bytes 1048600
  39.7 0.0 copy-start.5
  39.7 0.8 copy-done.5
  40.5 0.0 copy-start
  40.5 0.0 copy-start.1
  40.5 0.0 copy-start.2
  40.5 0.0 copy-start.3
  40.5 13.8 %attend_heads.1.res_ref = bf16[8,256,256]{2,1,0:T(8,128)(2,1)S(1)} custom-call(s32[8,8,128]{2,1,0:T(8,128)S(1)} %copy-done.5, bf16[8,256,256]{2,1,0:T(8,128)(2,1)S(1)} %copy-done.4), custom_call_target="tpu_custom_call" | custom-call | flops 6442450944 | bytes 83886080 | tf_op jit(solution)/shard_map/attend_heads/pallas_call | solution.py:583
  54.3 0.0 copy-done
  54.3 0.0 copy-done.1
  54.3 0.0 copy-done.2
  54.3 0.0 copy-done.3
  54.3 35.1 %collect_grads.1 = (bf16[256,512]{1,0:T(8,128)(2,1)S(1)}, bf16[8,192,128]{2,1,0:T(8,128)(2,1)S(1)}, bf16[2,256,512]{2,1,0:T(8,128)(2,1)S(1)}) custom-call(bf16[8,256,256]{2,1,0:T(8,128)(2,1)S(1)} %attend_heads.1.res_ref, bf16[8,4,64,1024]{3,2,1,0:T(8,128)(2,1)S(1)} %copy-done, bf16[1024,512]{1,0:T(8,128)(2,1)S(1)} %copy-done.1, ...), custom_call_target="tpu_custom_call" | custom-call | tf_op jit(solution)/shard_map/collect_grads/pallas_call | solution.py:728
  89.4 1.2 %finish.1 = (bf16[256,512]{1,0:T(8,128)(2,1)}, f32[256,512]{1,0:T(8,128)}, f32[128,512]{1,0:T(8,128)}, f32[128,512]{1,0:T(8,128)}, f32[128,512]{1,0:T(8,128)}) custom-call(bf16[256,512]{1,0:T(8,128)(2,1)S(1)} %get-tuple-element.14.att_in, bf16[8,192,128]{2,1,0:T(8,128)(2,1)S(1)} %get-tuple-element.15.terms, bf16[2,256,512]{2,1,0:T(8,128)(2,1)S(1)} %get-tuple-element.16.parts), custom_call_target="tpu_custom_call" | custom-call | tf_op jit(solution)/shard_map/finish/pallas_call | solution.py:748
Async XLA Ops:
  38.5 1.2 %copy-start.4 = (bf16[8,256,256]{2,1,0:T(8,128)(2,1)S(1)}, bf16[8,256,256]{2,1,0:T(8,128)(2,1)}, u32[]{:S(2)}) copy-start(bf16[8,256,256]{2,1,0:T(8,128)(2,1)} %get-tuple-element.12.heads_ref) | copy-start | bytes 3145732
  39.7 0.8 copy-start.5
  40.5 13.8 %copy-start = (bf16[8,4,64,1024]{3,2,1,0:T(8,128)(2,1)S(1)}, bf16[8,4,64,1024]{3,2,1,0:T(8,128)(2,1)}, u32[]{:S(2)}) copy-start(bf16[8,4,64,1024]{3,2,1,0:T(8,128)(2,1)} %get-tuple-element.13.x_ref) | copy-start | bytes 12582916
  40.5 13.8 %copy-start.1 = (bf16[1024,512]{1,0:T(8,128)(2,1)S(1)}, bf16[1024,512]{1,0:T(8,128)(2,1)}, u32[]{:S(2)}) copy-start(bf16[1024,512]{1,0:T(8,128)(2,1)} %wq_ref.3) | copy-start | bytes 3145732
  40.5 13.8 %copy-start.2 = (bf16[1024,512]{1,0:T(8,128)(2,1)S(1)}, bf16[1024,512]{1,0:T(8,128)(2,1)}, u32[]{:S(2)}) copy-start(bf16[1024,512]{1,0:T(8,128)(2,1)} %wk_ref.3) | copy-start | bytes 3145732
  40.5 13.8 %copy-start.3 = (bf16[1024,512]{1,0:T(8,128)(2,1)S(1)}, bf16[1024,512]{1,0:T(8,128)(2,1)}, u32[]{:S(2)}) copy-start(bf16[1024,512]{1,0:T(8,128)(2,1)} %wv_ref.3) | copy-start | bytes 3145732

commit v5 on v4

--- a/solution.py
+++ b/solution.py
@@ -213,7 +213,7 @@
 
 MESH = pl.DeviceIdType.MESH
 GROUP = 2
-CUTS = 2
+CUTS = 4
 
 
 def meet(axes):
@@ -652,10 +652,11 @@
         terms_out[peer, :DH] = term[:DH]
         terms_out[peer, DH:] = term[2 * DH :]
     terms_in[me] = terms_out[me]
-    for peer in peers:
+    for place, peer in enumerate(peers):
         res_copy(peer, peer).wait_recv()
-    for peer in peers:
-        term_copy(peer, me).start()
+        if place == len(peers) // 2:
+            for target in peers:
+                term_copy(target, me).start()
 
     def piece(which):
         return jnp.concatenate(

time: 91.7 us -> 92.3 us (level)
  no operation moved by 1% of the time
where the time goes in v5:
time: 92.3 us; the launch traced here: 91.5 us
  Pallas kernels  86.7 us (94%)
  local copies, waits for them, and re-layouts  1.99 us (2%)
  between operations  1.53 us (2%)
  other arithmetic  1.28 us (1%)
    pallas_call x1, Pallas kernels, spread(): pl.pallas_call(functools.partial(spread_kernel, n), out_shape=(jax.ShapeD...  36 us
    pallas_call x1, Pallas kernels, collect_grads(): pl.pallas_call(functools.partial(collect_kernel, n, n_row), out_shape=(ja...  34.9 us
    pallas_call x1, Pallas kernels, attend(): pl.pallas_call(functools.partial(attend_kernel, n, blocks), out_shape=jax...  14.7 us
    unnamed x12, local copies, waits for them, and re-layouts  1.99 us

profile of v5, /device:TPU:0, one launch (start us, length us, event | category | flops | bytes accessed | tf_op | source)
XLA Modules:
  0.0 91.5 jit_solution(14579179539063139290)
XLA Ops:
  1.3 1.3 %pad_select_fusion.code_ref = s32[8,128]{1,0:T(8,128)} fusion(s32[2,32]{1,0:T(2,128)} %bitcast.7, s32[]{:T(128)} %bitcast.5), kind=kLoop, calls=%fused_computation.1 | loop fusion | flops 2048 | bytes 4356 | tf_op jit(solution)/shard_map/concatenate | solution.py:777
  2.6 36.0 %spread_heads.1 = (bf16[8,256,256]{2,1,0:T(8,128)(2,1)}, s32[8,8,128]{2,1,0:T(8,128)}, bf16[8,8,32,1024]{3,2,1,0:T(8,128)(2,1)}) custom-call(bf16[8,32,1024]{2,1,0:T(8,128)(2,1)} %bitcast.6, bf16[1024,512]{1,0:T(8,128)(2,1)} %wq_ref.3, bf16[1024,512]{1,0:T(8,128)(2,1)} %wk_ref.3, bf16[1024,512]{1,0:T(8,128)(2,1)} %wv_ref.3, bf16[256,512]{1,0:T(8,128)(2,1)} %grad_ref.1, ...), custom_call_target="tpu_custom_call" | custom-call | flops 805306368 | bytes 41943040 | tf_op jit(solution)/shard_map/spread_heads/pallas_call | solution.py:432
  38.5 0.0 copy-start.4
  38.5 1.2 %copy-done.4 = bf16[8,256,256]{2,1,0:T(8,128)(2,1)S(1)} copy-done((bf16[8,256,256]{2,1,0:T(8,128)(2,1)S(1)}, bf16[8,256,256]{2,1,0:T(8,128)(2,1)}, u32[]{:S(2)}) %copy-start.4) | copy-done | bytes 1048600
  39.7 0.0 copy-start.5
  39.7 0.8 copy-done.5
  40.5 0.0 copy-start
  40.5 0.0 copy-start.1
  40.5 0.0 copy-start.2
  40.5 0.0 copy-start.3
  40.5 14.7 %attend_heads.1.res_ref = bf16[8,256,256]{2,1,0:T(8,128)(2,1)S(1)} custom-call(s32[8,8,128]{2,1,0:T(8,128)S(1)} %copy-done.5, bf16[8,256,256]{2,1,0:T(8,128)(2,1)S(1)} %copy-done.4), custom_call_target="tpu_custom_call" | custom-call | flops 6442450944 | bytes 83886080 | tf_op jit(solution)/shard_map/attend_heads/pallas_call | solution.py:583
  55.2 0.0 copy-done
  55.2 0.0 copy-done.1
  55.2 0.0 copy-done.2
  55.2 0.0 copy-done.3
  55.2 34.9 %collect_grads.1 = (bf16[256,512]{1,0:T(8,128)(2,1)S(1)}, bf16[8,192,128]{2,1,0:T(8,128)(2,1)S(1)}, bf16[2,256,512]{2,1,0:T(8,128)(2,1)S(1)}) custom-call(bf16[8,256,256]{2,1,0:T(8,128)(2,1)S(1)} %attend_heads.1.res_ref, bf16[8,8,32,1024]{3,2,1,0:T(8,128)(2,1)S(1)} %copy-done, bf16[1024,512]{1,0:T(8,128)(2,1)S(1)} %copy-done.1, ...), custom_call_target="tpu_custom_call" | custom-call | tf_op jit(solution)/shard_map/collect_grads/pallas_call | solution.py:729
  90.1 1.2 %finish.1 = (bf16[256,512]{1,0:T(8,128)(2,1)}, f32[256,512]{1,0:T(8,128)}, f32[128,512]{1,0:T(8,128)}, f32[128,512]{1,0:T(8,128)}, f32[128,512]{1,0:T(8,128)}) custom-call(bf16[256,512]{1,0:T(8,128)(2,1)S(1)} %get-tuple-element.14.att_in, bf16[8,192,128]{2,1,0:T(8,128)(2,1)S(1)} %get-tuple-element.15.terms, bf16[2,256,512]{2,1,0:T(8,128)(2,1)S(1)} %get-tuple-element.16.parts), custom_call_target="tpu_custom_call" | custom-call | tf_op jit(solution)/shard_map/finish/pallas_call | solution.py:749
Async XLA Ops:
  38.5 1.2 %copy-start.4 = (bf16[8,256,256]{2,1,0:T(8,128)(2,1)S(1)}, bf16[8,256,256]{2,1,0:T(8,128)(2,1)}, u32[]{:S(2)}) copy-start(bf16[8,256,256]{2,1,0:T(8,128)(2,1)} %get-tuple-element.12.heads_ref) | copy-start | bytes 3145732
  39.7 0.8 copy-start.5
  40.5 14.7 %copy-start = (bf16[8,8,32,1024]{3,2,1,0:T(8,128)(2,1)S(1)}, bf16[8,8,32,1024]{3,2,1,0:T(8,128)(2,1)}, u32[]{:S(2)}) copy-start(bf16[8,8,32,1024]{3,2,1,0:T(8,128)(2,1)} %get-tuple-element.13.x_ref) | copy-start | bytes 12582916
  40.5 14.7 %copy-start.1 = (bf16[1024,512]{1,0:T(8,128)(2,1)S(1)}, bf16[1024,512]{1,0:T(8,128)(2,1)}, u32[]{:S(2)}) copy-start(bf16[1024,512]{1,0:T(8,128)(2,1)} %wq_ref.3) | copy-start | bytes 3145732
  40.5 14.7 %copy-start.2 = (bf16[1024,512]{1,0:T(8,128)(2,1)S(1)}, bf16[1024,512]{1,0:T(8,128)(2,1)}, u32[]{:S(2)}) copy-start(bf16[1024,512]{1,0:T(8,128)(2,1)} %wk_ref.3) | copy-start | bytes 3145732
  40.5 14.7 %copy-start.3 = (bf16[1024,512]{1,0:T(8,128)(2,1)S(1)}, bf16[1024,512]{1,0:T(8,128)(2,1)}, u32[]{:S(2)}) copy-start(bf16[1024,512]{1,0:T(8,128)(2,1)} %wv_ref.3) | copy-start | bytes 3145732
